TPU v7x, 32 devices: a whole 2x2x4 slice. The times are simulated.
32 devices in a mesh: beam: 2 (over x), freq: 16 (over z, y, core).
Axes of the slice: x: 2, y: 2, z: 4, core: 2. Of those that a mesh axis runs over, the one named last changes fastest.
Arguments:
- spectra: float32 [512, 8192], P(('beam', 'freq')), parts along dimension 0, may hold values from -36 to 36
- profiles: bfloat16 [64, 256], replicated, may hold values from -0.375 to 0.375
- shifts: int32 [15, 32], replicated, may hold values from 0 to 512
Outputs:
- peaks: bfloat16 [512, 64, 64], P(('beam', 'freq')), parts along dimension 0
There are 2 independent parts, one for each index of `beam`. A program takes and returns all parts, laid end to end along the dimension named above; an argument that names none is the same for every part. Nothing has to cross between parts.
All inputs are finite; a program needn't handle non-finite values.
Results may differ from a plain program's by a relative error of at most 0.0048.
Values sent between devices are 32-bit elements; how exact they have to be, the bound alone decides.
No kernel may reach another device: no remote copies, remote signals or barrier semaphores. Data moves between devices by JAX's collectives and lax.ppermute only.
A program may use at most 64 MiB of HBM per device.

v0:
```python
import functools

import jax
import jax.numpy as jnp
from jax import lax
from jax.experimental import pallas as pl
from jax.experimental.pallas import tpu as pltpu
from jax.sharding import PartitionSpec as P

STRIDE = 8
HOLD = 16
LANES = 128
HALO = 8
VMEM_LIMIT = 48 * 1024 * 1024


def reversed_bits(value, count):
    result = 0
    for bit in range(count):
        result |= ((value >> bit) & 1) << (count - 1 - bit)
    return result


def pack_kernel(x_ref, msg_ref):
    row_count, time_len = x_ref.shape
    block_count = time_len // LANES
    stride = block_count + HALO
    power = jnp.zeros((8, LANES), jnp.float32)
    for column in range(block_count):
        for half in range(row_count // 8):
            piece = x_ref[half * 8 : half * 8 + 8, column * LANES : (column + 1) * LANES]
            power = power + piece * piece
            msg_ref[pl.ds(half * 8 * stride + column, 8, stride=stride), :] = piece
    for row in range(row_count):
        msg_ref[row * stride + block_count : (row + 1) * stride, :] = power


def tree_levels(first, second, shifts_ref, index, low_bit, bit_count, subband_count, row_count, block_count):
    row_bits = row_count.bit_length() - 1
    stride = block_count + HALO
    lane = lax.broadcasted_iota(jnp.int32, (block_count, LANES), 1)
    own = [(index >> (low_bit + k)) & 1 for k in range(bit_count)]
    source, target = first, second
    for k in range(bit_count):
        level = low_bit + k
        sources = 1 << (row_bits - bit_count + k)
        base = 0
        for q in range(k + 1, bit_count):
            base = base + (own[q] << (row_bits - 1 - (q - k - 1)))
        column = own[k] * row_count + base
        for group in range(1 << (bit_count - k - 1)):
            node = (
                subband_count
                - (subband_count >> level)
                + ((index >> (low_bit + bit_count)) << (bit_count - k - 1))
                + group
            )
            for row in range(2 * sources):
                if k == 0:
                    low = reversed_bits(2 * group, bit_count) * sources + row // 2
                    high = reversed_bits(2 * group + 1, bit_count) * sources + row // 2
                else:
                    low = 2 * group * sources + row // 2
                    high = low + sources
                delay = shifts_ref[node, column + row]
                lines, part = delay >> 7, delay & (LANES - 1)
                at = high * stride + HALO
                near = source[pl.ds(at - lines, block_count), :]
                far = source[pl.ds(at - lines - 1, block_count), :]
                moved = pltpu.roll(jnp.where(lane < LANES - part, near, far), part, 1)
                kept = source[low * stride + HALO : (low + 1) * stride, :]
                slot = (group * 2 * sources + row) * stride + HALO
                target[slot : slot + block_count, :] = kept + moved
        source, target = target, source
    return source


def unpack(msg_ref, first, second, row_count, block_count, per_message):
    stride = block_count + HALO
    span = per_message * block_count + HALO
    zeros = jnp.zeros((HALO, LANES), jnp.float32)
    power = zeros
    for scratch in (first, second):
        for row in range(row_count + 1):
            scratch[row * stride : row * stride + HALO, :] = zeros
    for message in range(row_count // per_message):
        for part in range(per_message):
            row = message * per_message + part
            first[row * stride + HALO : (row + 1) * stride, :] = msg_ref[
                message * span + part * block_count : message * span + (part + 1) * block_count, :
            ]
        power = power + msg_ref[message * span + per_message * block_count : (message + 1) * span, :]
    return power


def merge_kernel(low_bit, bit_count, next_bits, subband_count, row_count, block_count, shifts_ref, msg_ref, out_ref, first, second):
    index = lax.axis_index("freq")
    stride = block_count + HALO
    power = unpack(msg_ref, first, second, row_count, block_count, row_count >> bit_count)
    final = tree_levels(first, second, shifts_ref, index, low_bit, bit_count, subband_count, row_count, block_count)
    per_message = row_count >> next_bits
    span = per_message * block_count + HALO
    for message in range(1 << next_bits):
        for part in range(per_message):
            row = message * per_message + part
            out_ref[message * span + part * block_count : message * span + (part + 1) * block_count, :] = final[
                row * stride + HALO : (row + 1) * stride, :
            ]
        out_ref[message * span + per_message * block_count : (message + 1) * span, :] = power


def final_kernel(
    low_bit, bit_count, subband_count, row_count, block_count, shifts_ref, prof_ref, msg_ref, out_ref,
    first, second, windows, table,
):
    index = lax.axis_index("freq")
    stride = block_count + HALO
    prof_count, tap_count = prof_ref.shape
    span_len = table.shape[1]
    blocks = span_len // LANES
    power = unpack(msg_ref, first, second, row_count, block_count, row_count >> bit_count)
    profiles = jnp.concatenate(
        [prof_ref[...].astype(jnp.float32), jnp.zeros((prof_count, span_len - tap_count), jnp.float32)], axis=1
    )
    for offset in range(HOLD):
        moved = profiles if offset == 0 else pltpu.roll(profiles, offset * STRIDE, 1)
        table[offset * prof_count : (offset + 1) * prof_count, :] = moved.astype(jnp.bfloat16)
    final = tree_levels(first, second, shifts_ref, index, low_bit, bit_count, subband_count, row_count, block_count)
    for row in range(row_count):
        for block in range(blocks):
            at = row * stride + HALO + block
            windows[row * block_count : (row + 1) * block_count, block * LANES : (block + 1) * LANES] = final[
                at : at + block_count, :
            ].astype(jnp.bfloat16)
    total = jnp.sum(jnp.sum(power, axis=0, keepdims=True), axis=1, keepdims=True)
    samples = subband_count * row_count * block_count * LANES
    rms_level = jnp.sqrt(subband_count * total / samples + 1e-06)
    group = 256 // block_count
    for start in range(0, row_count, group):
        products = lax.dot_general(
            table[...],
            windows[start * block_count : (start + group) * block_count, :],
            (((1,), (1,)), ((), ())),
            preferred_element_type=jnp.float32,
        )
        best = products[:prof_count]
        for offset in range(1, HOLD):
            best = jnp.maximum(best, products[offset * prof_count : (offset + 1) * prof_count])
        best = best / rms_level
        for row in range(group):
            out_ref[start + row] = best[:, row * block_count : (row + 1) * block_count].astype(jnp.bfloat16)


def stage_groups(subband_count, low_bit, bit_count):
    groups = []
    for rest in range(subband_count >> bit_count):
        low = rest & ((1 << low_bit) - 1)
        high = rest >> low_bit
        groups.append(
            [
                low + (reversed_bits(slot, bit_count) << low_bit) + (high << (low_bit + bit_count))
                for slot in range(1 << bit_count)
            ]
        )
    return groups


def per_device(spectra, profiles, shifts):
    row_count, time_len = spectra.shape
    prof_count, tap_count = profiles.shape
    subband_count = lax.axis_size("freq")
    level_count = subband_count.bit_length() - 1
    row_bits = row_count.bit_length() - 1
    block_count = time_len // LANES
    stages = []
    while sum(stages) < level_count:
        stages.append(min(row_bits, level_count - sum(stages)))
    vmem = pl.BlockSpec(memory_space=pltpu.VMEM)
    smem = pl.BlockSpec(memory_space=pltpu.SMEM)
    params = pltpu.CompilerParams(vmem_limit_bytes=VMEM_LIMIT)
    states = [pltpu.VMEM(((row_count + 1) * (block_count + HALO), LANES), jnp.float32)] * 2

    def message_shape(bit_count):
        return jax.ShapeDtypeStruct(((row_count * block_count + (HALO << bit_count)), LANES), jnp.float32)

    messages = pl.pallas_call(
        pack_kernel,
        out_shape=message_shape(stages[0]),
        in_specs=[vmem],
        out_specs=vmem,
        compiler_params=params,
    )(spectra)
    low_bit = 0
    for number, bit_count in enumerate(stages):
        shape = messages.shape
        messages = lax.all_to_all(
            messages.reshape(1 << bit_count, -1, LANES),
            "freq",
            0,
            0,
            tiled=True,
            axis_index_groups=stage_groups(subband_count, low_bit, bit_count),
        ).reshape(shape)
        sizes = (subband_count, row_count, block_count)
        if number + 1 < len(stages):
            next_bits = stages[number + 1]
            messages = pl.pallas_call(
                functools.partial(merge_kernel, low_bit, bit_count, next_bits, *sizes),
                out_shape=message_shape(next_bits),
                in_specs=[smem, vmem],
                out_specs=vmem,
                scratch_shapes=states,
                compiler_params=params,
            )(shifts, messages)
        low_bit += bit_count
    block_len = STRIDE * HOLD
    extra = (tap_count + block_len - STRIDE - 1) // block_len
    span_len = (extra + 1) * block_len
    return pl.pallas_call(
        functools.partial(final_kernel, low_bit - bit_count, bit_count, *sizes),
        out_shape=jax.ShapeDtypeStruct((row_count, prof_count, block_count), jnp.bfloat16),
        in_specs=[smem, vmem, vmem],
        out_specs=vmem,
        scratch_shapes=states
        + [
            pltpu.VMEM((row_count * block_count, span_len), jnp.bfloat16),
            pltpu.VMEM((HOLD * prof_count, span_len), jnp.bfloat16),
        ],
        compiler_params=params,
    )(shifts, profiles, messages)


def solution(mesh):
    in_specs = (P(("beam", "freq"), None), P(), P())
    out_specs = P(("beam", "freq"), None, None)
    return jax.shard_map(
        per_device, mesh=mesh, in_specs=in_specs, out_specs=out_specs, check_vma=False
    )
```

profile of v0, /device:TPU:0, one launch (start us, length us, event | category | flops | bytes accessed | tf_op | source)
XLA Modules:
  0.0 29.5 jit_solution(14964897630291241025)
XLA Ops:
  0.0 0.0 copy-start
  0.0 1.0 %copy-done = f32[16,8192]{1,0:T(8,128)S(1)} copy-done((f32[16,8192]{1,0:T(8,128)S(1)}, f32[16,8192]{1,0:T(8,128)}, u32[]{:S(2)}) %copy-start) | copy-done | bytes 524312
  1.0 0.2 shard_map.37
  1.2 0.0 copy-start.1
  1.2 0.0 copy-start.2
  1.2 24.7 %all_to_all.5 = f32[16,72,128]{2,1,0:T(8,128)S(1)} all-to-all(f32[16,72,128]{2,1,0:T(8,128)S(1)} %bitcast.3), channel_id=1, replica_groups={{0,8,4,12,2,10,6,14,1,9,5,13,3,11,7,15},{16,24,20,28,18,26,22,30,17,25,..., dimensions={0} | all-to-all | bytes 1179648 | tf_op jit(solution)/shard_map/all_to_all | solution.py:196
  25.9 0.0 copy-done.1
  25.9 0.0 copy-done.2
  25.9 3.6 %shard_map.38 = bf16[16,64,64]{2,1,0:T(8,128)(2,1)} custom-call(s32[15,32]{1,0:T(8,128)S(1)} %copy-done.2, bf16[64,256]{1,0:T(8,128)(2,1)S(1)} %copy-done.1, f32[1152,128]{1,0:T(8,128)S(1)} %bitcast.2), custom_call_target="tpu_custom_call" | custom-call | tf_op jit(solution)/shard_map/pallas_call | solution.py:219
Async XLA Ops:
  0.0 1.0 %copy-start = (f32[16,8192]{1,0:T(8,128)S(1)}, f32[16,8192]{1,0:T(8,128)}, u32[]{:S(2)}) copy-start(f32[16,8192]{1,0:T(8,128)} %x_ref.1) | copy-start | bytes 1572868
  1.2 24.7 %copy-start.1 = (bf16[64,256]{1,0:T(8,128)(2,1)S(1)}, bf16[64,256]{1,0:T(8,128)(2,1)}, u32[]{:S(2)}) copy-start(bf16[64,256]{1,0:T(8,128)(2,1)} %prof_ref.1) | copy-start | bytes 98308
  1.2 24.7 %copy-start.2 = (s32[15,32]{1,0:T(8,128)S(1)}, s32[15,32]{1,0:T(8,128)}, u32[]{:S(2)}) copy-start(s32[15,32]{1,0:T(8,128)} %shifts_ref.1) | copy-start | bytes 5764
where the time goes:
time: 29.8 us; the launch traced here: 29.5 us
  blocking collectives  24.7 us (83%)
  Pallas kernels  3.8 us (13%)
  local copies, waits for them, and re-layouts  1.05 us (4%)
    all_to_all x1, blocking collectives, per_device(): lax.all_to_all(messages.reshape(1 << bit_count, -1, LANES), 'freq', 0, 0,...  24.7 us
    pallas_call x1, Pallas kernels, per_device(): pl.pallas_call(functools.partial(final_kernel, low_bit - bit_count, bit_c...  3.62 us
    unnamed x6, local copies, waits for them, and re-layouts  1.05 us

commit v1 on v0

v1 whole, which is shorter than its diff:
```python
import functools
import itertools

import jax
import jax.numpy as jnp
from jax import lax
from jax.experimental import pallas as pl
from jax.experimental.pallas import tpu as pltpu
from jax.sharding import PartitionSpec as P

STRIDE = 8
HOLD = 16
LANES = 128
HALO = 8
VMEM_LIMIT = 48 * 1024 * 1024
RAW_MASKS = (4, 5)
MERGED_MASKS = (6, 7, 2, 3, 1)


def reversed_bits(value, count):
    result = 0
    for bit in range(count):
        result |= ((value >> bit) & 1) << (count - 1 - bit)
    return result


def lines_at(start, count):
    return pl.ds(pl.multiple_of(start, 8), count)


def pack_rows(x_ref, store):
    row_count, time_len = x_ref.shape
    power = jnp.zeros((8, LANES), jnp.float32)
    for column in range(time_len // LANES):
        for half in range(row_count // 8):
            piece = x_ref[half * 8 : half * 8 + 8, column * LANES : (column + 1) * LANES]
            power = power + piece * piece
            store(half, column, piece)
    return power


def pack_kernel(x_ref, msg_ref):
    row_count, time_len = x_ref.shape
    block_count = time_len // LANES
    stride = HALO + block_count

    def store(half, column, piece):
        msg_ref[pl.ds(half * 8 * stride + HALO + column, 8, stride=stride), :] = piece

    power = pack_rows(x_ref, store)
    for row in range(row_count):
        msg_ref[row * stride : row * stride + HALO, :] = power


def split_kernel(x_ref, *refs):
    raw_refs, (sent_ref, kept_ref) = refs[:-2], refs[-2:]
    index = lax.axis_index("freq")
    core, chip = index & 1, (index >> 1) & 7
    row_count, time_len = x_ref.shape
    block_count = time_len // LANES
    half_span = row_count // 2 * block_count

    def body(own_half):
        def store(half, column, piece):
            ref = kept_ref if half == own_half else sent_ref
            ref[pl.ds(HALO + column, 8, stride=block_count), :] = piece

        power = pack_rows(x_ref, store)
        kept_ref[:HALO, :] = power
        sent_ref[:HALO, :] = power
        for number, mask in enumerate(RAW_MASKS):
            place = reversed_bits(chip ^ mask, 3)
            for flip, ref in enumerate((kept_ref, sent_ref)):
                out_ref = raw_refs[2 * number + flip]
                out_ref[HALO:, :] = ref[lines_at(HALO + place * block_count, block_count), :]
                out_ref[:HALO, :] = power

    for own_half in range(2):
        pl.when(core == own_half)(functools.partial(body, own_half))


def delayed(source, high, delay, block_count):
    lane = lax.broadcasted_iota(jnp.int32, (block_count, LANES), 1)
    line = lax.broadcasted_iota(jnp.int32, (HALO, LANES), 0)
    lines, part = delay >> 7, delay & (LANES - 1)
    near = source[pl.ds(high - lines, block_count), :]
    far = source[pl.ds(high - lines - 1, block_count), :]
    moved = pltpu.roll(jnp.where(lane < LANES - part, near, far), part, 1)
    head = jnp.where(line * LANES + lane[:HALO] >= delay, moved[:HALO], 0.0)
    return jnp.concatenate([head, moved[HALO:]], axis=0)


def core_merge_kernel(block_count, row_count, shifts_ref, got_ref, kept_ref, *outs):
    index = lax.axis_index("freq")
    core, chip = index & 1, (index >> 1) & 7

    def body(low_ref, high_ref):
        power = low_ref[:HALO, :] + high_ref[:HALO, :]
        for mask, out_ref in zip((0,) + MERGED_MASKS, outs):
            place = reversed_bits(chip ^ mask, 3)
            at = HALO + place * block_count
            for part in range(2):
                delay = shifts_ref[index >> 1, core * row_count + 2 * place + part]
                out_ref[HALO + part * block_count : HALO + (part + 1) * block_count, :] = low_ref[
                    lines_at(at, block_count), :
                ] + delayed(high_ref, at, delay, block_count)
            out_ref[:HALO, :] = power

    pl.when(core == 0)(lambda: body(kept_ref, got_ref))
    pl.when(core == 1)(lambda: body(got_ref, kept_ref))


def tree_levels(first, second, shifts_ref, index, low_bit, bit_count, subband_count, row_count, block_count):
    row_bits = row_count.bit_length() - 1
    own = [(index >> (low_bit + k)) & 1 for k in range(bit_count)]
    source, target = first, second
    for k in range(bit_count):
        level = low_bit + k
        sources = 1 << (row_bits - bit_count + k)
        base = 0
        for q in range(k + 1, bit_count):
            base = base + (own[q] << (row_bits - 1 - (q - k - 1)))
        column = own[k] * row_count + base
        for group in range(1 << (bit_count - k - 1)):
            node = (
                subband_count
                - (subband_count >> level)
                + ((index >> (low_bit + bit_count)) << (bit_count - k - 1))
                + group
            )
            for row in range(2 * sources):
                low = 2 * group * sources + row // 2
                high = low + sources
                at = HALO + (group * 2 * sources + row) * block_count
                target[at : at + block_count, :] = source[
                    HALO + low * block_count : HALO + (low + 1) * block_count, :
                ] + delayed(source, HALO + high * block_count, shifts_ref[node, column + row], block_count)
        source, target = target, source
    return source


def gather_messages(sizes, low_bit, bit_count, msg_refs, first, second, shifts_ref):
    subband_count, row_count, block_count = sizes
    index = lax.axis_index("freq")
    power = jnp.zeros((HALO, LANES), jnp.float32)
    if len(msg_refs) > 1:
        core, chip = index & 1, (index >> 1) & 7
        count = 1 + len(MERGED_MASKS)
        merged, raw = msg_refs[:count], msg_refs[count:]
        for number, mask in enumerate(RAW_MASKS):
            for flip in range(2):
                ref = raw[2 * number + flip]
                at = HALO + (2 * number + (core ^ flip)) * block_count
                second[lines_at(at, block_count), :] = ref[HALO:, :]
                power = power + ref[:HALO, :]
        for number, mask in enumerate(RAW_MASKS):
            low = HALO + 2 * number * block_count
            for part in range(2):
                delay = shifts_ref[(index >> 1) ^ mask, core * row_count + 2 * reversed_bits(chip, 3) + part]
                at = HALO + (2 * (chip ^ mask) + part) * block_count
                first[lines_at(at, block_count), :] = second[low : low + block_count, :] + delayed(
                    second, low + block_count, delay, block_count
                )
        for mask, ref in zip((0,) + MERGED_MASKS, merged):
            at = HALO + 2 * (chip ^ mask) * block_count
            first[lines_at(at, 2 * block_count), :] = ref[HALO:, :]
            power = power + ref[:HALO, :]
        low_bit, bit_count = low_bit + 1, bit_count - 1
    else:
        (msg_ref,) = msg_refs
        span = (row_count >> bit_count) * block_count
        for message in range(1 << bit_count):
            at = HALO + reversed_bits(message, bit_count) * span
            start = message * (HALO + span)
            power = power + msg_ref[start : start + HALO, :]
            first[at : at + span, :] = msg_ref[start + HALO : start + HALO + span, :]
    final = tree_levels(first, second, shifts_ref, index, low_bit, bit_count, *sizes)
    return final, power


def merge_kernel(sizes, low_bit, bit_count, next_bits, shifts_ref, *refs):
    msg_refs, (out_ref, first, second) = refs[:-3], refs[-3:]
    _, row_count, block_count = sizes
    final, power = gather_messages(sizes, low_bit, bit_count, msg_refs, first, second, shifts_ref)
    span = (row_count >> next_bits) * block_count
    for message in range(1 << next_bits):
        start = message * (HALO + span)
        out_ref[start : start + HALO, :] = power
        out_ref[start + HALO : start + HALO + span, :] = final[HALO + message * span : HALO + (message + 1) * span, :]


def final_kernel(sizes, low_bit, bit_count, shifts_ref, prof_ref, *refs):
    msg_refs, (out_ref, first, second, windows, table) = refs[:-5], refs[-5:]
    subband_count, row_count, block_count = sizes
    prof_count, tap_count = prof_ref.shape
    span_len = table.shape[1]
    profiles = jnp.concatenate(
        [prof_ref[...].astype(jnp.float32), jnp.zeros((prof_count, span_len - tap_count), jnp.float32)], axis=1
    )
    for offset in range(HOLD):
        moved = profiles if offset == 0 else pltpu.roll(profiles, offset * STRIDE, 1)
        table[offset * prof_count : (offset + 1) * prof_count, :] = moved.astype(jnp.bfloat16)
    final, power = gather_messages(sizes, low_bit, bit_count, msg_refs, first, second, shifts_ref)
    line = lax.broadcasted_iota(jnp.int32, (block_count, LANES), 0)
    for row in range(row_count):
        for block in range(span_len // LANES):
            at = HALO + row * block_count + block
            piece = final[at : at + block_count, :]
            if block:
                piece = jnp.where(line < block_count - block, piece, 0.0)
            windows[row * block_count : (row + 1) * block_count, block * LANES : (block + 1) * LANES] = piece.astype(
                jnp.bfloat16
            )
    total = jnp.sum(jnp.sum(power, axis=0, keepdims=True), axis=1, keepdims=True)
    samples = subband_count * row_count * block_count * LANES
    rms_level = jnp.sqrt(subband_count * total / samples + 1e-06)
    group = 256 // block_count
    for start in range(0, row_count, group):
        products = lax.dot_general(
            table[...],
            windows[start * block_count : (start + group) * block_count, :],
            (((1,), (1,)), ((), ())),
            preferred_element_type=jnp.float32,
        )
        best = products[:prof_count]
        for offset in range(1, HOLD):
            best = jnp.maximum(best, products[offset * prof_count : (offset + 1) * prof_count])
        best = best / rms_level
        for row in range(group):
            out_ref[start + row] = best[:, row * block_count : (row + 1) * block_count].astype(jnp.bfloat16)


def stage_groups(subband_count, low_bit, bit_count):
    groups = []
    for rest in range(subband_count >> bit_count):
        low = rest & ((1 << low_bit) - 1)
        high = rest >> low_bit
        groups.append(
            [
                low + (reversed_bits(slot, bit_count) << low_bit) + (high << (low_bit + bit_count))
                for slot in range(1 << bit_count)
            ]
        )
    return groups


def exchange(value, mask):
    return lax.ppermute(value, "freq", [(source, source ^ mask) for source in range(lax.axis_size("freq"))])


def call(kernel, out_shape, in_specs, args, scratch=()):
    vmem = pl.BlockSpec(memory_space=pltpu.VMEM)
    return pl.pallas_call(
        kernel,
        out_shape=out_shape,
        in_specs=in_specs,
        out_specs=jax.tree.map(lambda _: vmem, out_shape),
        scratch_shapes=list(scratch),
        compiler_params=pltpu.CompilerParams(vmem_limit_bytes=VMEM_LIMIT),
    )(*args)


def per_device(spectra, profiles, shifts):
    row_count, time_len = spectra.shape
    prof_count, tap_count = profiles.shape
    subband_count = lax.axis_size("freq")
    level_count = subband_count.bit_length() - 1
    row_bits = row_count.bit_length() - 1
    block_count = time_len // LANES
    sizes = (subband_count, row_count, block_count)
    stages = []
    while sum(stages) < level_count:
        stages.append(min(row_bits, level_count - sum(stages)))
    vmem = pl.BlockSpec(memory_space=pltpu.VMEM)
    smem = pl.BlockSpec(memory_space=pltpu.SMEM)
    states = [pltpu.VMEM((row_count * block_count + 2 * HALO, LANES), jnp.float32)] * 2

    def lines(rows, tiles=1):
        return jax.ShapeDtypeStruct((rows * block_count + tiles * HALO, LANES), jnp.float32)

    def all_to_all(messages, low_bit, bit_count):
        shape = messages.shape
        pieces = messages.reshape(1 << bit_count, -1, LANES)
        groups = stage_groups(subband_count, low_bit, bit_count)
        return lax.all_to_all(pieces, "freq", 0, 0, tiled=True, axis_index_groups=groups).reshape(shape)

    if stages[0] == 4 and row_count == 16:
        half = row_count // 2
        *raw, sent, kept = call(
            split_kernel, [lines(1)] * (2 * len(RAW_MASKS)) + [lines(half)] * 2, [vmem], (spectra,)
        )
        got = exchange(sent, 1)
        raw = [exchange(value, 2 * mask + flip) for value, (mask, flip) in zip(raw, itertools.product(RAW_MASKS, (0, 1)))]
        own, *merged = call(
            functools.partial(core_merge_kernel, block_count, row_count),
            [lines(2)] * (1 + len(MERGED_MASKS)),
            [smem, vmem, vmem],
            (shifts, got, kept),
        )
        merged = [exchange(value, 2 * mask) for value, mask in zip(merged, MERGED_MASKS)]
        messages = [own, *merged, *raw]
    else:
        packed = call(pack_kernel, lines(row_count, 1 << stages[0]), [vmem], (spectra,))
        messages = [all_to_all(packed, 0, stages[0])]
    low_bit = 0
    for bit_count, next_bits in zip(stages[:-1], stages[1:]):
        packed = call(
            functools.partial(merge_kernel, sizes, low_bit, bit_count, next_bits),
            lines(row_count, 1 << next_bits),
            [smem] + [vmem] * len(messages),
            (shifts, *messages),
            states,
        )
        low_bit += bit_count
        messages = [all_to_all(packed, low_bit, next_bits)]
    block_len = STRIDE * HOLD
    extra = (tap_count + block_len - STRIDE - 1) // block_len
    span_len = (extra + 1) * block_len
    return call(
        functools.partial(final_kernel, sizes, low_bit, stages[-1]),
        jax.ShapeDtypeStruct((row_count, prof_count, block_count), jnp.bfloat16),
        [smem] + [vmem] * (1 + len(messages)),
        (shifts, profiles, *messages),
        states
        + [
            pltpu.VMEM((row_count * block_count, span_len), jnp.bfloat16),
            pltpu.VMEM((HOLD * prof_count, span_len), jnp.bfloat16),
        ],
    )


def solution(mesh):
    in_specs = (P(("beam", "freq"), None), P(), P())
    out_specs = P(("beam", "freq"), None, None)
    return jax.shard_map(
        per_device, mesh=mesh, in_specs=in_specs, out_specs=out_specs, check_vma=False
    )
```

time: 29.8 us -> 27 us (0.906)
  blocking collectives: 24.7 us -> 0 us
  starting transfers between devices: 0 us -> 16.1 us
  waiting for transfers between devices: 0 us -> 4.85 us
  Pallas kernels: 3.8 us -> 4.82 us
    all_to_all x1 -> x0, blocking collectives: 24.7 us -> none  [per_device(): lax.all_to_all(messages.reshape(1 << bit_count, -1, LANES), 'freq', 0, 0,...]
    ppermute x0 -> x10, starting transfers between devices: none -> 16.1 us  [exchange(): lax.ppermute(value, 'freq', [(source, source ^ mask) for source in range(...]
    ppermute x0 -> x10, waiting for transfers between devices: none -> 4.85 us  [exchange(): lax.ppermute(value, 'freq', [(source, source ^ mask) for source in range(...]
    pallas_call x2 -> x3, Pallas kernels: 3.8 us -> 4.82 us  [call(): pl.pallas_call(kernel, out_shape=out_shape, in_specs=in_specs, out_specs=...]
  transfers between devices with their start and end apart: 0 -> 10, of which waited for: 0 -> 3; matrix products, arithmetic and copies ran while one was open for 0% -> 0% of each run, Pallas kernels for 0% -> 3%
where the time goes in v1:
time: 27 us; the launch traced here: 26.9 us
  starting transfers between devices  16.1 us (60%)
  waiting for transfers between devices  4.85 us (18%)
  Pallas kernels  4.82 us (18%)
  local copies, waits for them, and re-layouts  1.05 us (4%)
    ppermute x10, starting transfers between devices, exchange(): lax.ppermute(value, 'freq', [(source, source ^ mask) for source in range(...  16.1 us
    ppermute x10, waiting for transfers between devices, exchange(): lax.ppermute(value, 'freq', [(source, source ^ mask) for source in range(...  4.85 us
    pallas_call x3, Pallas kernels, call(): pl.pallas_call(kernel, out_shape=out_shape, in_specs=in_specs, out_specs=...  4.82 us
    unnamed x6, local copies, waits for them, and re-layouts  1.05 us
  transfers between devices with their start and end apart: 10, of which 3 were waited for; matrix products, arithmetic and copies ran while one was open for 0% of the time, Pallas kernels for 3%

profile of v1, /device:TPU:0, one launch (start us, length us, event | category | flops | bytes accessed | tf_op | source)
XLA Modules:
  0.0 26.9 jit_solution(8038758060666863726)
XLA Ops:
  0.0 0.0 copy-start
  0.0 1.0 %copy-done = f32[16,8192]{1,0:T(8,128)S(1)} copy-done((f32[16,8192]{1,0:T(8,128)S(1)}, f32[16,8192]{1,0:T(8,128)}, u32[]{:S(2)}) %copy-start) | copy-done | bytes 524312
  1.0 0.4 %shard_map.37 = (f32[72,128]{1,0:T(8,128)S(1)}, f32[72,128]{1,0:T(8,128)S(1)}, f32[72,128]{1,0:T(8,128)S(1)}, f32[72,128]{1,0:T(8,128)S(1)}, f32[520,128]{1,0:T(8,128)S(1)}, /*index=5*/f32[520,128]{1,0:T(8,128)S(1)}) custom-call(f32[16,8192]{1,0:T(8,128)S(1)} %copy-done), custom_call_target="tpu_custom_call" | custom-call | tf_op jit(solution)/shard_map/pallas_call | solution.py:253
  1.5 0.0 copy-start.1
  1.5 0.5 %collective-permute-start = (f32[520,128]{1,0:T(8,128)S(1)}, f32[520,128]{1,0:T(8,128)S(1)}, u32[]{:S(2)}, u32[]{:S(2)}) collective-permute-start(f32[520,128]{1,0:T(8,128)S(1)} %get-tuple-element.17), channel_id=1, source_target_pairs={{0,1},{1,0},{2,3},{3,2},{4,5},{5,4},{6,7},{7,6},{8,9},{9,8},{10,11... | collective-permute-start | bytes 798728 | tf_op jit(solution)/shard_map/ppermute | solution.py:248
  2.0 3.7 %collective-permute-start.6 = (f32[72,128]{1,0:T(8,128)S(1)}, f32[72,128]{1,0:T(8,128)S(1)}, u32[]{:S(2)}, u32[]{:S(2)}) collective-permute-start(f32[72,128]{1,0:T(8,128)S(1)} %get-tuple-element.25), channel_id=1, source_target_pairs={{0,8},{1,9},{2,10},{3,11},{4,12},{5,13},{6,14},{7,15},{8,0},{9,1},... | collective-permute-start | bytes 110600 | tf_op jit(solution)/shard_map/ppermute | solution.py:248
  5.7 0.1 collective-permute-start.7
  5.7 3.6 %collective-permute-start.8 = (f32[72,128]{1,0:T(8,128)S(1)}, f32[72,128]{1,0:T(8,128)S(1)}, u32[]{:S(2)}, u32[]{:S(2)}) collective-permute-start(f32[72,128]{1,0:T(8,128)S(1)} %get-tuple-element.27), channel_id=1, source_target_pairs={{0,10},{1,11},{2,8},{3,9},{4,14},{5,15},{6,12},{7,13},{8,2},{9,3},... | collective-permute-start | bytes 110600 | tf_op jit(solution)/shard_map/ppermute | solution.py:248
  9.3 0.0 collective-permute-start.9
  9.3 0.0 collective-permute-done.got_ref
  9.3 0.0 copy-done.1
  9.3 0.0 copy-start.2
  9.3 0.9 %shard_map.38 = (f32[136,128]{1,0:T(8,128)S(1)}, f32[136,128]{1,0:T(8,128)S(1)}, f32[136,128]{1,0:T(8,128)S(1)}, f32[136,128]{1,0:T(8,128)S(1)}, f32[136,128]{1,0:T(8,128)S(1)}, /*index=5*/f32[136,128]{1,0:T(8,128)S(1)}) custom-call(s32[15,32]{1,0:T(8,128)S(1)} %copy-done.1, f32[520,128]{1,0:T(8,128)S(1)} %collective-permute-done.got_ref, ...), custom_call_target="tpu_custom_call" | custom-call | tf_op jit(solution)/shard_map/pallas_call | solution.py:253
  10.2 3.6 %collective-permute-start.1 = (f32[136,128]{1,0:T(8,128)S(1)}, f32[136,128]{1,0:T(8,128)S(1)}, u32[]{:S(2)}, u32[]{:S(2)}) collective-permute-start(f32[136,128]{1,0:T(8,128)S(1)} %get-tuple-element.20), channel_id=1, source_target_pairs={{0,12},{1,13},{2,14},{3,15},{4,8},{5,9},{6,10},{7,11},{8,4},{9,5},... | collective-permute-start | bytes 208904 | tf_op jit(solution)/shard_map/ppermute | solution.py:248
  13.8 0.0 collective-permute-done.6.refs_6_
  13.8 1.2 %collective-permute-start.2 = (f32[136,128]{1,0:T(8,128)S(1)}, f32[136,128]{1,0:T(8,128)S(1)}, u32[]{:S(2)}, u32[]{:S(2)}) collective-permute-start(f32[136,128]{1,0:T(8,128)S(1)} %get-tuple-element.21), channel_id=1, source_target_pairs={{0,14},{1,15},{2,12},{3,13},{4,10},{5,11},{6,8},{7,9},{8,6},{9,7},... | collective-permute-start | bytes 208904 | tf_op jit(solution)/shard_map/ppermute | solution.py:248
  15.0 0.0 collective-permute-done.7.refs_7_
  15.0 0.0 collective-permute-start.3
  15.0 0.0 collective-permute-done.8.refs_8_
  15.0 2.1 %collective-permute-start.4 = (f32[136,128]{1,0:T(8,128)S(1)}, f32[136,128]{1,0:T(8,128)S(1)}, u32[]{:S(2)}, u32[]{:S(2)}) collective-permute-start(f32[136,128]{1,0:T(8,128)S(1)} %get-tuple-element.23), channel_id=1, source_target_pairs={{0,6},{1,7},{2,4},{3,5},{4,2},{5,3},{6,0},{7,1},{8,14},{9,15},{10,... | collective-permute-start | bytes 208904 | tf_op jit(solution)/shard_map/ppermute | solution.py:248
  17.0 0.0 collective-permute-done.9.refs_9_
  17.1 1.4 %collective-permute-start.5 = (f32[136,128]{1,0:T(8,128)S(1)}, f32[136,128]{1,0:T(8,128)S(1)}, u32[]{:S(2)}, u32[]{:S(2)}) collective-permute-start(f32[136,128]{1,0:T(8,128)S(1)} %get-tuple-element.24), channel_id=1, source_target_pairs={{0,2},{1,3},{2,0},{3,1},{4,6},{5,7},{6,4},{7,5},{8,10},{9,11},{10,... | collective-permute-start | bytes 208904 | tf_op jit(solution)/shard_map/ppermute | solution.py:248
  18.5 0.0 collective-permute-done.1.refs_1_
  18.5 3.0 %collective-permute-done.2.refs_2_ = f32[136,128]{1,0:T(8,128)S(1)} collective-permute-done((f32[136,128]{1,0:T(8,128)S(1)}, f32[136,128]{1,0:T(8,128)S(1)}, u32[]{:S(2)}, u32[]{:S(2)}) %collective-permute-start.2) | collective-permute-done | bytes 69664 | tf_op jit(solution)/shard_map/ppermute | solution.py:248
  21.5 0.0 collective-permute-done.3.refs_3_
  21.5 0.9 %collective-permute-done.4.refs_4_ = f32[136,128]{1,0:T(8,128)S(1)} collective-permute-done((f32[136,128]{1,0:T(8,128)S(1)}, f32[136,128]{1,0:T(8,128)S(1)}, u32[]{:S(2)}, u32[]{:S(2)}) %collective-permute-start.4) | collective-permute-done | bytes 69664 | tf_op jit(solution)/shard_map/ppermute | solution.py:248
  22.4 1.0 %collective-permute-done.5.refs_5_ = f32[136,128]{1,0:T(8,128)S(1)} collective-permute-done((f32[136,128]{1,0:T(8,128)S(1)}, f32[136,128]{1,0:T(8,128)S(1)}, u32[]{:S(2)}, u32[]{:S(2)}) %collective-permute-start.5) | collective-permute-done | bytes 69664 | tf_op jit(solution)/shard_map/ppermute | solution.py:248
  23.3 0.0 copy-done.2
  23.3 3.5 %shard_map.39 = bf16[16,64,64]{2,1,0:T(8,128)(2,1)} custom-call(s32[15,32]{1,0:T(8,128)S(1)} %copy-done.1, bf16[64,256]{1,0:T(8,128)(2,1)S(1)} %copy-done.2, f32[136,128]{1,0:T(8,128)S(1)} %get-tuple-element.19.refs_0_, f32[136,128]{1,0:T(8,128)S(1)} %collective-permute-done.1.refs_1_, f32[136,128]{1,0:T(8,128)S(1)} %collective-permute-done.2.refs_2_, ...), custom_call_target="tpu_custom_call" | custom-call | tf_op jit(solution)/shard_map/pallas_call | solution.py:253
Async XLA Ops:
  0.0 1.0 %copy-start = (f32[16,8192]{1,0:T(8,128)S(1)}, f32[16,8192]{1,0:T(8,128)}, u32[]{:S(2)}) copy-start(f32[16,8192]{1,0:T(8,128)} %x_ref.1) | copy-start | bytes 1572868
  1.5 7.9 %copy-start.1 = (s32[15,32]{1,0:T(8,128)S(1)}, s32[15,32]{1,0:T(8,128)}, u32[]{:S(2)}) copy-start(s32[15,32]{1,0:T(8,128)} %shifts_ref.3) | copy-start | bytes 5764
  1.5 7.9 %collective-permute-start = (f32[520,128]{1,0:T(8,128)S(1)}, f32[520,128]{1,0:T(8,128)S(1)}, u32[]{:S(2)}, u32[]{:S(2)}) collective-permute-start(f32[520,128]{1,0:T(8,128)S(1)} %get-tuple-element.17), channel_id=1, source_target_pairs={{0,1},{1,0},{2,3},{3,2},{4,5},{5,4},{6,7},{7,6},{8,9},{9,8},{10,11... | collective-permute-start | bytes 798728 | tf_op jit(solution)/shard_map/ppermute | solution.py:248
  2.0 11.8 %collective-permute-start.6 = (f32[72,128]{1,0:T(8,128)S(1)}, f32[72,128]{1,0:T(8,128)S(1)}, u32[]{:S(2)}, u32[]{:S(2)}) collective-permute-start(f32[72,128]{1,0:T(8,128)S(1)} %get-tuple-element.25), channel_id=1, source_target_pairs={{0,8},{1,9},{2,10},{3,11},{4,12},{5,13},{6,14},{7,15},{8,0},{9,1},... | collective-permute-start | bytes 110600 | tf_op jit(solution)/shard_map/ppermute | solution.py:248
  5.7 9.3 %collective-permute-start.7 = (f32[72,128]{1,0:T(8,128)S(1)}, f32[72,128]{1,0:T(8,128)S(1)}, u32[]{:S(2)}, u32[]{:S(2)}) collective-permute-start(f32[72,128]{1,0:T(8,128)S(1)} %get-tuple-element.26), channel_id=1, source_target_pairs={{0,9},{1,8},{2,11},{3,10},{4,13},{5,12},{6,15},{7,14},{8,1},{9,0},... | collective-permute-start | bytes 110600 | tf_op jit(solution)/shard_map/ppermute | solution.py:248
  5.7 9.3 %collective-permute-start.8 = (f32[72,128]{1,0:T(8,128)S(1)}, f32[72,128]{1,0:T(8,128)S(1)}, u32[]{:S(2)}, u32[]{:S(2)}) collective-permute-start(f32[72,128]{1,0:T(8,128)S(1)} %get-tuple-element.27), channel_id=1, source_target_pairs={{0,10},{1,11},{2,8},{3,9},{4,14},{5,15},{6,12},{7,13},{8,2},{9,3},... | collective-permute-start | bytes 110600 | tf_op jit(solution)/shard_map/ppermute | solution.py:248
  9.3 7.7 %collective-permute-start.9 = (f32[72,128]{1,0:T(8,128)S(1)}, f32[72,128]{1,0:T(8,128)S(1)}, u32[]{:S(2)}, u32[]{:S(2)}) collective-permute-start(f32[72,128]{1,0:T(8,128)S(1)} %get-tuple-element.28), channel_id=1, source_target_pairs={{0,11},{1,10},{2,9},{3,8},{4,15},{5,14},{6,13},{7,12},{8,3},{9,2},... | collective-permute-start | bytes 110600 | tf_op jit(solution)/shard_map/ppermute | solution.py:248
  9.3 14.0 %copy-start.2 = (bf16[64,256]{1,0:T(8,128)(2,1)S(1)}, bf16[64,256]{1,0:T(8,128)(2,1)}, u32[]{:S(2)}) copy-start(bf16[64,256]{1,0:T(8,128)(2,1)} %prof_ref.1) | copy-start | bytes 98308
  10.2 8.3 %collective-permute-start.1 = (f32[136,128]{1,0:T(8,128)S(1)}, f32[136,128]{1,0:T(8,128)S(1)}, u32[]{:S(2)}, u32[]{:S(2)}) collective-permute-start(f32[136,128]{1,0:T(8,128)S(1)} %get-tuple-element.20), channel_id=1, source_target_pairs={{0,12},{1,13},{2,14},{3,15},{4,8},{5,9},{6,10},{7,11},{8,4},{9,5},... | collective-permute-start | bytes 208904 | tf_op jit(solution)/shard_map/ppermute | solution.py:248
  13.8 7.7 %collective-permute-start.2 = (f32[136,128]{1,0:T(8,128)S(1)}, f32[136,128]{1,0:T(8,128)S(1)}, u32[]{:S(2)}, u32[]{:S(2)}) collective-permute-start(f32[136,128]{1,0:T(8,128)S(1)} %get-tuple-element.21), channel_id=1, source_target_pairs={{0,14},{1,15},{2,12},{3,13},{4,10},{5,11},{6,8},{7,9},{8,6},{9,7},... | collective-permute-start | bytes 208904 | tf_op jit(solution)/shard_map/ppermute | solution.py:248
  15.0 6.5 %collective-permute-start.3 = (f32[136,128]{1,0:T(8,128)S(1)}, f32[136,128]{1,0:T(8,128)S(1)}, u32[]{:S(2)}, u32[]{:S(2)}) collective-permute-start(f32[136,128]{1,0:T(8,128)S(1)} %get-tuple-element.22), channel_id=1, source_target_pairs={{0,4},{1,5},{2,6},{3,7},{4,0},{5,1},{6,2},{7,3},{8,12},{9,13},{10,... | collective-permute-start | bytes 208904 | tf_op jit(solution)/shard_map/ppermute | solution.py:248
  15.0 7.4 %collective-permute-start.4 = (f32[136,128]{1,0:T(8,128)S(1)}, f32[136,128]{1,0:T(8,128)S(1)}, u32[]{:S(2)}, u32[]{:S(2)}) collective-permute-start(f32[136,128]{1,0:T(8,128)S(1)} %get-tuple-element.23), channel_id=1, source_target_pairs={{0,6},{1,7},{2,4},{3,5},{4,2},{5,3},{6,0},{7,1},{8,14},{9,15},{10,... | collective-permute-start | bytes 208904 | tf_op jit(solution)/shard_map/ppermute | solution.py:248
  17.1 6.3 %collective-permute-start.5 = (f32[136,128]{1,0:T(8,128)S(1)}, f32[136,128]{1,0:T(8,128)S(1)}, u32[]{:S(2)}, u32[]{:S(2)}) collective-permute-start(f32[136,128]{1,0:T(8,128)S(1)} %get-tuple-element.24), channel_id=1, source_target_pairs={{0,2},{1,3},{2,0},{3,1},{4,6},{5,7},{6,4},{7,5},{8,10},{9,11},{10,... | collective-permute-start | bytes 208904 | tf_op jit(solution)/shard_map/ppermute | solution.py:248

commit v2 on v1

--- a/solution.py
+++ b/solution.py
@@ -1,5 +1,4 @@
 import functools
-import itertools
 
 import jax
 import jax.numpy as jnp
@@ -13,8 +12,9 @@
 LANES = 128
 HALO = 8
 VMEM_LIMIT = 48 * 1024 * 1024
-RAW_MASKS = (4, 5)
-MERGED_MASKS = (6, 7, 2, 3, 1)
+RAW_MASKS = (7, 6)
+MERGED_MASKS = (5, 4, 3, 2, 1)
+AFTER = 2
 
 
 def reversed_bits(value, count):
@@ -69,11 +69,11 @@
         kept_ref[:HALO, :] = power
         sent_ref[:HALO, :] = power
         for number, mask in enumerate(RAW_MASKS):
-            place = reversed_bits(chip ^ mask, 3)
-            for flip, ref in enumerate((kept_ref, sent_ref)):
-                out_ref = raw_refs[2 * number + flip]
-                out_ref[HALO:, :] = ref[lines_at(HALO + place * block_count, block_count), :]
-                out_ref[:HALO, :] = power
+            at = HALO + reversed_bits(chip ^ mask, 3) * block_count
+            out_ref = raw_refs[number]
+            out_ref[:HALO, :] = power
+            out_ref[HALO : HALO + block_count, :] = sent_ref[lines_at(at, block_count), :]
+            out_ref[HALO + block_count :, :] = kept_ref[lines_at(at, block_count), :]
 
     for own_half in range(2):
         pl.when(core == own_half)(functools.partial(body, own_half))
@@ -108,6 +108,16 @@
 
     pl.when(core == 0)(lambda: body(kept_ref, got_ref))
     pl.when(core == 1)(lambda: body(got_ref, kept_ref))
+
+
+def pass_kernel(block_count, *refs):
+    raw_refs, out_ref = refs[: len(RAW_MASKS)], refs[-1]
+    power = raw_refs[0][:HALO, :]
+    for ref in raw_refs[1:]:
+        power = power + ref[:HALO, :]
+    out_ref[:HALO, :] = power
+    for number, ref in enumerate(raw_refs):
+        out_ref[HALO + number * block_count : HALO + (number + 1) * block_count, :] = ref[HALO : HALO + block_count, :]
 
 
 def tree_levels(first, second, shifts_ref, index, low_bit, bit_count, subband_count, row_count, block_count):
@@ -146,13 +156,18 @@
     if len(msg_refs) > 1:
         core, chip = index & 1, (index >> 1) & 7
         count = 1 + len(MERGED_MASKS)
-        merged, raw = msg_refs[:count], msg_refs[count:]
+        merged, raw, passed_refs = msg_refs[:count], msg_refs[count : count + len(RAW_MASKS)], msg_refs[count + len(RAW_MASKS) :]
         for number, mask in enumerate(RAW_MASKS):
-            for flip in range(2):
-                ref = raw[2 * number + flip]
-                at = HALO + (2 * number + (core ^ flip)) * block_count
-                second[lines_at(at, block_count), :] = ref[HALO:, :]
-                power = power + ref[:HALO, :]
+            ref = raw[number]
+            at = HALO + (2 * number + core) * block_count
+            second[lines_at(at, block_count), :] = ref[HALO + block_count :, :]
+            at = HALO + (2 * number + 1 - core) * block_count
+            second[lines_at(at, block_count), :] = passed_refs[0][
+                HALO + number * block_count : HALO + (number + 1) * block_count, :
+            ]
+            power = power + ref[:HALO, :]
+        if RAW_MASKS:
+            power = power + passed_refs[0][:HALO, :]
         for number, mask in enumerate(RAW_MASKS):
             low = HALO + 2 * number * block_count
             for part in range(2):
@@ -287,10 +302,10 @@
     if stages[0] == 4 and row_count == 16:
         half = row_count // 2
         *raw, sent, kept = call(
-            split_kernel, [lines(1)] * (2 * len(RAW_MASKS)) + [lines(half)] * 2, [vmem], (spectra,)
-        )
+            split_kernel, [lines(2)] * len(RAW_MASKS) + [lines(half)] * 2, [vmem], (spectra,)
+        )
+        raw = [exchange(value, 2 * mask) for value, mask in zip(raw, RAW_MASKS)]
         got = exchange(sent, 1)
-        raw = [exchange(value, 2 * mask + flip) for value, (mask, flip) in zip(raw, itertools.product(RAW_MASKS, (0, 1)))]
         own, *merged = call(
             functools.partial(core_merge_kernel, block_count, row_count),
             [lines(2)] * (1 + len(MERGED_MASKS)),
@@ -299,6 +314,14 @@
         )
         merged = [exchange(value, 2 * mask) for value, mask in zip(merged, MERGED_MASKS)]
         messages = [own, *merged, *raw]
+        if RAW_MASKS:
+            passed = call(
+                functools.partial(pass_kernel, block_count),
+                lines(len(RAW_MASKS)),
+                [vmem] * (1 + len(RAW_MASKS)),
+                (*raw, merged[AFTER]),
+            )
+            messages.append(exchange(passed, 1))
     else:
         packed = call(pack_kernel, lines(row_count, 1 << stages[0]), [vmem], (spectra,))
         messages = [all_to_all(packed, 0, stages[0])]

time: 27 us -> 23.7 us (0.88)
  starting transfers between devices: 16.1 us -> 12.7 us
    ppermute x10 -> x9, starting transfers between devices: 16.1 us -> 12.7 us  [exchange(): lax.ppermute(value, 'freq', [(source, source ^ mask) for source in range(...]
    ppermute x10 -> x9, waiting for transfers between devices: 4.85 us -> 4.92 us  [exchange(): lax.ppermute(value, 'freq', [(source, source ^ mask) for source in range(...]
    pallas_call x3 -> x4, Pallas kernels: 4.82 us -> 4.83 us  [call(): pl.pallas_call(kernel, out_shape=out_shape, in_specs=in_specs, out_specs=...]
  transfers between devices with their start and end apart: 10 -> 9, of which waited for: 3 -> 3; matrix products, arithmetic and copies ran while one was open for 0% -> 0% of each run, Pallas kernels for 3% -> 4%
where the time goes in v2:
time: 23.7 us; the launch traced here: 23.6 us
  starting transfers between devices  12.7 us (54%)
  waiting for transfers between devices  4.92 us (21%)
  Pallas kernels  4.83 us (20%)
  local copies, waits for them, and re-layouts  1.05 us (4%)
    ppermute x9, starting transfers between devices, exchange(): lax.ppermute(value, 'freq', [(source, source ^ mask) for source in range(...  12.7 us
    ppermute x9, waiting for transfers between devices, exchange(): lax.ppermute(value, 'freq', [(source, source ^ mask) for source in range(...  4.92 us
    pallas_call x4, Pallas kernels, call(): pl.pallas_call(kernel, out_shape=out_shape, in_specs=in_specs, out_specs=...  4.83 us
    unnamed x6, local copies, waits for them, and re-layouts  1.05 us
  transfers between devices with their start and end apart: 9, of which 3 were waited for; matrix products, arithmetic and copies ran while one was open for 0% of the time, Pallas kernels for 4%

profile of v2, /device:TPU:0, one launch (start us, length us, event | category | flops | bytes accessed | tf_op | source)
XLA Modules:
  0.0 23.6 jit_solution(6868813630000404903)
XLA Ops:
  0.0 0.0 copy-start
  0.0 1.0 %copy-done = f32[16,8192]{1,0:T(8,128)S(1)} copy-done((f32[16,8192]{1,0:T(8,128)S(1)}, f32[16,8192]{1,0:T(8,128)}, u32[]{:S(2)}) %copy-start) | copy-done | bytes 524312
  1.0 0.0 copy-start.1
  1.0 0.4 %shard_map.37 = (f32[136,128]{1,0:T(8,128)S(1)}, f32[136,128]{1,0:T(8,128)S(1)}, f32[520,128]{1,0:T(8,128)S(1)}, f32[520,128]{1,0:T(8,128)S(1)}) custom-call(f32[16,8192]{1,0:T(8,128)S(1)} %copy-done), custom_call_target="tpu_custom_call" | custom-call | tf_op jit(solution)/shard_map/pallas_call | solution.py:268
  1.5 0.5 %collective-permute-start = (f32[520,128]{1,0:T(8,128)S(1)}, f32[520,128]{1,0:T(8,128)S(1)}, u32[]{:S(2)}, u32[]{:S(2)}) collective-permute-start(f32[520,128]{1,0:T(8,128)S(1)} %get-tuple-element.15), channel_id=1, source_target_pairs={{0,1},{1,0},{2,3},{3,2},{4,5},{5,4},{6,7},{7,6},{8,9},{9,8},{10,11... | collective-permute-start | bytes 798728 | tf_op jit(solution)/shard_map/ppermute | solution.py:263
  2.0 5.6 %collective-permute-start.6 = (f32[136,128]{1,0:T(8,128)S(1)}, f32[136,128]{1,0:T(8,128)S(1)}, u32[]{:S(2)}, u32[]{:S(2)}) collective-permute-start(f32[136,128]{1,0:T(8,128)S(1)} %get-tuple-element.23), channel_id=1, source_target_pairs={{0,14},{1,15},{2,12},{3,13},{4,10},{5,11},{6,8},{7,9},{8,6},{9,7},... | collective-permute-start | bytes 208904 | tf_op jit(solution)/shard_map/ppermute | solution.py:263
  7.6 0.2 collective-permute-start.7
  7.8 0.0 collective-permute-done.got_ref
  7.8 0.0 copy-done.1
  7.8 0.9 %shard_map.38 = (f32[136,128]{1,0:T(8,128)S(1)}, f32[136,128]{1,0:T(8,128)S(1)}, f32[136,128]{1,0:T(8,128)S(1)}, f32[136,128]{1,0:T(8,128)S(1)}, f32[136,128]{1,0:T(8,128)S(1)}, /*index=5*/f32[136,128]{1,0:T(8,128)S(1)}) custom-call(s32[15,32]{1,0:T(8,128)S(1)} %copy-done.1, f32[520,128]{1,0:T(8,128)S(1)} %collective-permute-done.got_ref, ...), custom_call_target="tpu_custom_call" | custom-call | tf_op jit(solution)/shard_map/pallas_call | solution.py:268
  8.7 0.1 collective-permute-start.3
  8.8 5.1 %collective-permute-start.1 = (f32[136,128]{1,0:T(8,128)S(1)}, f32[136,128]{1,0:T(8,128)S(1)}, u32[]{:S(2)}, u32[]{:S(2)}) collective-permute-start(f32[136,128]{1,0:T(8,128)S(1)} %get-tuple-element.18), channel_id=1, source_target_pairs={{0,10},{1,11},{2,8},{3,9},{4,14},{5,15},{6,12},{7,13},{8,2},{9,3},... | collective-permute-start | bytes 208904 | tf_op jit(solution)/shard_map/ppermute | solution.py:263
  13.8 0.0 collective-permute-start.2
  13.8 0.0 collective-permute-done.6.refs_0_.refs_6_
  13.8 0.8 %collective-permute-start.4 = (f32[136,128]{1,0:T(8,128)S(1)}, f32[136,128]{1,0:T(8,128)S(1)}, u32[]{:S(2)}, u32[]{:S(2)}) collective-permute-start(f32[136,128]{1,0:T(8,128)S(1)} %get-tuple-element.21), channel_id=1, source_target_pairs={{0,4},{1,5},{2,6},{3,7},{4,0},{5,1},{6,2},{7,3},{8,12},{9,13},{10,... | collective-permute-start | bytes 208904 | tf_op jit(solution)/shard_map/ppermute | solution.py:263
  14.6 0.0 collective-permute-done.7.refs_1_.refs_7_
  14.6 0.0 copy-start.2
  14.6 0.4 %collective-permute-start.5 = (f32[136,128]{1,0:T(8,128)S(1)}, f32[136,128]{1,0:T(8,128)S(1)}, u32[]{:S(2)}, u32[]{:S(2)}) collective-permute-start(f32[136,128]{1,0:T(8,128)S(1)} %get-tuple-element.22), channel_id=1, source_target_pairs={{0,2},{1,3},{2,0},{3,1},{4,6},{5,7},{6,4},{7,5},{8,10},{9,11},{10,... | collective-permute-start | bytes 208904 | tf_op jit(solution)/shard_map/ppermute | solution.py:263
  15.1 1.1 %collective-permute-done.3.refs_2_.refs_3_ = f32[136,128]{1,0:T(8,128)S(1)} collective-permute-done((f32[136,128]{1,0:T(8,128)S(1)}, f32[136,128]{1,0:T(8,128)S(1)}, u32[]{:S(2)}, u32[]{:S(2)}) %collective-permute-start.3) | collective-permute-done | bytes 69664 | tf_op jit(solution)/shard_map/ppermute | solution.py:263
  16.1 0.0 collective-permute-start.8
  16.2 3.3 %collective-permute-done.1.refs_1_ = f32[136,128]{1,0:T(8,128)S(1)} collective-permute-done((f32[136,128]{1,0:T(8,128)S(1)}, f32[136,128]{1,0:T(8,128)S(1)}, u32[]{:S(2)}, u32[]{:S(2)}) %collective-permute-start.1) | collective-permute-done | bytes 69664 | tf_op jit(solution)/shard_map/ppermute | solution.py:263
  19.4 0.6 %collective-permute-done.2.refs_2_ = f32[136,128]{1,0:T(8,128)S(1)} collective-permute-done((f32[136,128]{1,0:T(8,128)S(1)}, f32[136,128]{1,0:T(8,128)S(1)}, u32[]{:S(2)}, u32[]{:S(2)}) %collective-permute-start.2) | collective-permute-done | bytes 69664 | tf_op jit(solution)/shard_map/ppermute | solution.py:263
  20.0 0.0 collective-permute-done.4.refs_4_
  20.0 0.0 collective-permute-done.5.refs_5_
  20.0 0.0 collective-permute-done.8.refs_8_
  20.0 0.0 copy-done.2
  20.0 3.6 %shard_map.40 = bf16[16,64,64]{2,1,0:T(8,128)(2,1)} custom-call(s32[15,32]{1,0:T(8,128)S(1)} %copy-done.1, bf16[64,256]{1,0:T(8,128)(2,1)S(1)} %copy-done.2, f32[136,128]{1,0:T(8,128)S(1)} %get-tuple-element.17.refs_0_, f32[136,128]{1,0:T(8,128)S(1)} %collective-permute-done.1.refs_1_, f32[136,128]{1,0:T(8,128)S(1)} %collective-permute-done.2.refs_2_, ...), custom_call_target="tpu_custom_call" | custom-call | tf_op jit(solution)/shard_map/pallas_call | solution.py:268
  (1 shorter events, 0.0 us)
Async XLA Ops:
  0.0 1.0 %copy-start = (f32[16,8192]{1,0:T(8,128)S(1)}, f32[16,8192]{1,0:T(8,128)}, u32[]{:S(2)}) copy-start(f32[16,8192]{1,0:T(8,128)} %x_ref.1) | copy-start | bytes 1572868
  1.0 6.8 %copy-start.1 = (s32[15,32]{1,0:T(8,128)S(1)}, s32[15,32]{1,0:T(8,128)}, u32[]{:S(2)}) copy-start(s32[15,32]{1,0:T(8,128)} %shifts_ref.3) | copy-start | bytes 5764
  1.5 6.4 %collective-permute-start = (f32[520,128]{1,0:T(8,128)S(1)}, f32[520,128]{1,0:T(8,128)S(1)}, u32[]{:S(2)}, u32[]{:S(2)}) collective-permute-start(f32[520,128]{1,0:T(8,128)S(1)} %get-tuple-element.15), channel_id=1, source_target_pairs={{0,1},{1,0},{2,3},{3,2},{4,5},{5,4},{6,7},{7,6},{8,9},{9,8},{10,11... | collective-permute-start | bytes 798728 | tf_op jit(solution)/shard_map/ppermute | solution.py:263
  2.0 11.9 %collective-permute-start.6 = (f32[136,128]{1,0:T(8,128)S(1)}, f32[136,128]{1,0:T(8,128)S(1)}, u32[]{:S(2)}, u32[]{:S(2)}) collective-permute-start(f32[136,128]{1,0:T(8,128)S(1)} %get-tuple-element.23), channel_id=1, source_target_pairs={{0,14},{1,15},{2,12},{3,13},{4,10},{5,11},{6,8},{7,9},{8,6},{9,7},... | collective-permute-start | bytes 208904 | tf_op jit(solution)/shard_map/ppermute | solution.py:263
  7.6 7.0 %collective-permute-start.7 = (f32[136,128]{1,0:T(8,128)S(1)}, f32[136,128]{1,0:T(8,128)S(1)}, u32[]{:S(2)}, u32[]{:S(2)}) collective-permute-start(f32[136,128]{1,0:T(8,128)S(1)} %get-tuple-element.24), channel_id=1, source_target_pairs={{0,12},{1,13},{2,14},{3,15},{4,8},{5,9},{6,10},{7,11},{8,4},{9,5},... | collective-permute-start | bytes 208904 | tf_op jit(solution)/shard_map/ppermute | solution.py:263
  8.7 7.4 %collective-permute-start.3 = (f32[136,128]{1,0:T(8,128)S(1)}, f32[136,128]{1,0:T(8,128)S(1)}, u32[]{:S(2)}, u32[]{:S(2)}) collective-permute-start(f32[136,128]{1,0:T(8,128)S(1)} %get-tuple-element.20), channel_id=1, source_target_pairs={{0,6},{1,7},{2,4},{3,5},{4,2},{5,3},{6,0},{7,1},{8,14},{9,15},{10,... | collective-permute-start | bytes 208904 | tf_op jit(solution)/shard_map/ppermute | solution.py:263
  8.8 10.6 %collective-permute-start.1 = (f32[136,128]{1,0:T(8,128)S(1)}, f32[136,128]{1,0:T(8,128)S(1)}, u32[]{:S(2)}, u32[]{:S(2)}) collective-permute-start(f32[136,128]{1,0:T(8,128)S(1)} %get-tuple-element.18), channel_id=1, source_target_pairs={{0,10},{1,11},{2,8},{3,9},{4,14},{5,15},{6,12},{7,13},{8,2},{9,3},... | collective-permute-start | bytes 208904 | tf_op jit(solution)/shard_map/ppermute | solution.py:263
  13.8 6.2 %collective-permute-start.2 = (f32[136,128]{1,0:T(8,128)S(1)}, f32[136,128]{1,0:T(8,128)S(1)}, u32[]{:S(2)}, u32[]{:S(2)}) collective-permute-start(f32[136,128]{1,0:T(8,128)S(1)} %get-tuple-element.19), channel_id=1, source_target_pairs={{0,8},{1,9},{2,10},{3,11},{4,12},{5,13},{6,14},{7,15},{8,0},{9,1},... | collective-permute-start | bytes 208904 | tf_op jit(solution)/shard_map/ppermute | solution.py:263
  13.8 6.2 %collective-permute-start.4 = (f32[136,128]{1,0:T(8,128)S(1)}, f32[136,128]{1,0:T(8,128)S(1)}, u32[]{:S(2)}, u32[]{:S(2)}) collective-permute-start(f32[136,128]{1,0:T(8,128)S(1)} %get-tuple-element.21), channel_id=1, source_target_pairs={{0,4},{1,5},{2,6},{3,7},{4,0},{5,1},{6,2},{7,3},{8,12},{9,13},{10,... | collective-permute-start | bytes 208904 | tf_op jit(solution)/shard_map/ppermute | solution.py:263
  14.6 5.4 %copy-start.2 = (bf16[64,256]{1,0:T(8,128)(2,1)S(1)}, bf16[64,256]{1,0:T(8,128)(2,1)}, u32[]{:S(2)}) copy-start(bf16[64,256]{1,0:T(8,128)(2,1)} %prof_ref.1) | copy-start | bytes 98308
  14.6 5.4 %collective-permute-start.5 = (f32[136,128]{1,0:T(8,128)S(1)}, f32[136,128]{1,0:T(8,128)S(1)}, u32[]{:S(2)}, u32[]{:S(2)}) collective-permute-start(f32[136,128]{1,0:T(8,128)S(1)} %get-tuple-element.22), channel_id=1, source_target_pairs={{0,2},{1,3},{2,0},{3,1},{4,6},{5,7},{6,4},{7,5},{8,10},{9,11},{10,... | collective-permute-start | bytes 208904 | tf_op jit(solution)/shard_map/ppermute | solution.py:263
  16.1 3.9 %collective-permute-start.8 = (f32[136,128]{1,0:T(8,128)S(1)}, f32[136,128]{1,0:T(8,128)S(1)}, u32[]{:S(2)}, u32[]{:S(2)}) collective-permute-start(f32[136,128]{1,0:T(8,128)S(1)} %shard_map.39), channel_id=1, source_target_pairs={{0,1},{1,0},{2,3},{3,2},{4,5},{5,4},{6,7},{7,6},{8,9},{9,8},{10,11... | collective-permute-start | bytes 208904 | tf_op jit(solution)/shard_map/ppermute | solution.py:263

commit v3 on v1

v3 whole, which is shorter than its diff:
```python
import functools

import jax
import jax.numpy as jnp
from jax import lax
from jax.experimental import pallas as pl
from jax.experimental.pallas import tpu as pltpu
from jax.sharding import PartitionSpec as P

STRIDE = 8
HOLD = 16
LANES = 128
HALO = 8
VMEM_LIMIT = 48 * 1024 * 1024
FETCHES = 4
RAW_MASKS = (7, 5)
MERGED_MASKS = (4, 6, 3, 2, 1)
PASS_AFTER = 3


def reversed_bits(value, count):
    result = 0
    for bit in range(count):
        result |= ((value >> bit) & 1) << (count - 1 - bit)
    return result


def lines_at(start, count):
    return pl.ds(pl.multiple_of(start, 8), count)


def aligned_rows(x_ref, buffer, sems, store):
    row_count, time_len = x_ref.shape
    width = time_len // FETCHES
    copies = []
    for part in range(FETCHES):
        for half in range(row_count // 8):
            at = (pl.ds(half * 8, 8), pl.ds(part * width, width))
            copies.append(pltpu.make_async_copy(x_ref.at[at], buffer.at[at], sems.at[len(copies)]))
    for copy in copies:
        copy.start()
    power = jnp.zeros((8, LANES), jnp.float32)
    for part in range(FETCHES):
        for half in range(row_count // 8):
            copies[part * (row_count // 8) + half].wait()
            for column in range(part * width // LANES, (part + 1) * width // LANES):
                piece = buffer[half * 8 : half * 8 + 8, column * LANES : (column + 1) * LANES]
                power = power + piece * piece
                store(half, column, piece)
    return power


def pack_kernel(x_ref, msg_ref, buffer, sems):
    row_count, time_len = x_ref.shape
    block_count = time_len // LANES
    stride = HALO + block_count

    def store(half, column, piece):
        msg_ref[pl.ds(half * 8 * stride + HALO + column, 8, stride=stride), :] = piece

    power = aligned_rows(x_ref, buffer, sems, store)
    for row in range(row_count):
        msg_ref[row * stride : row * stride + HALO, :] = power


def split_kernel(x_ref, *refs):
    raw_refs, (sent_ref, kept_ref, rows, buffer, sems) = refs[:-5], refs[-5:]
    index = lax.axis_index("freq")
    core, chip = index & 1, (index >> 1) & 7
    row_count, time_len = x_ref.shape
    block_count = time_len // LANES
    half_rows = row_count // 2
    stride = block_count + HALO

    def store(half, column, piece):
        rows[pl.ds(half * 8 * stride + column, 8, stride=stride), :] = piece

    power = aligned_rows(x_ref, buffer, sems, store)
    for ref in (*raw_refs, sent_ref, kept_ref):
        ref[:HALO, :] = power
    sent_at, kept_at = (1 - core) * half_rows * stride, core * half_rows * stride
    for mask, out_ref in zip(RAW_MASKS, raw_refs):
        at = reversed_bits(chip ^ mask, 3) * stride
        out_ref[HALO : HALO + block_count, :] = rows[lines_at(sent_at + at, block_count), :]
        out_ref[HALO + block_count :, :] = rows[lines_at(kept_at + at, block_count), :]
    for row in range(half_rows):
        for ref, at in ((sent_ref, sent_at), (kept_ref, kept_at)):
            ref[HALO + row * block_count : HALO + (row + 1) * block_count, :] = rows[
                lines_at(at + row * stride, block_count), :
            ]


def delays_at(shifts_ref, node, groups, column, count):
    rows = shifts_ref[pl.ds(node, groups), :]
    rows = jnp.concatenate([rows, jnp.zeros((groups, LANES - rows.shape[1]), jnp.int32)], axis=1)
    rows = pltpu.roll(rows, (LANES - column) & (LANES - 1), 1)
    return [[rows[group, row] for row in range(count)] for group in range(groups)]


def delayed(source, high, delay, block_count):
    lane = lax.broadcasted_iota(jnp.int32, (block_count, LANES), 1)
    line = lax.broadcasted_iota(jnp.int32, (HALO, LANES), 0)
    lines, part = delay >> 7, delay & (LANES - 1)
    near = source[pl.ds(high - lines, block_count), :]
    far = source[pl.ds(high - lines - 1, block_count), :]
    moved = pltpu.roll(jnp.where(lane < LANES - part, near, far), part, 1)
    head = jnp.where(line * LANES + lane[:HALO] >= delay, moved[:HALO], 0.0)
    return jnp.concatenate([head, moved[HALO:]], axis=0)


def merge(source, low, high, delays, target, at, block_count, rows=None):
    for row in range(len(delays)) if rows is None else rows:
        skip = row // 2 * block_count
        target[lines_at(at + row * block_count, block_count), :] = source[
            lines_at(low + skip, block_count), :
        ] + delayed(source, high + skip, delays[row], block_count)


def core_merge_kernel(block_count, row_count, shifts_ref, got_ref, kept_ref, *outs):
    index = lax.axis_index("freq")
    core, chip = index & 1, (index >> 1) & 7
    row = jnp.broadcast_to(shifts_ref[pl.ds(index >> 1, 1), :], (row_count, 2 * row_count))
    entry = lax.broadcasted_iota(jnp.int32, row.shape, 0) ^ (2 * reversed_bits(chip, 3))
    column = lax.broadcasted_iota(jnp.int32, row.shape, 1)
    picked = jnp.where(column == entry + core * row_count, row.astype(jnp.float32), 0.0)
    picked = jnp.sum(picked, axis=1, keepdims=True).astype(jnp.int32)

    def body(low_ref, high_ref):
        power = low_ref[:HALO, :] + high_ref[:HALO, :]
        for mask, out_ref in zip((0,) + MERGED_MASKS, outs):
            at = HALO + reversed_bits(chip ^ mask, 3) * block_count
            for part in range(2):
                delay = picked[2 * reversed_bits(mask, 3) + part, 0]
                out_ref[HALO + part * block_count : HALO + (part + 1) * block_count, :] = low_ref[
                    lines_at(at, block_count), :
                ] + delayed(high_ref, at, delay, block_count)
            out_ref[:HALO, :] = power

    pl.when(core == 0)(lambda: body(kept_ref, got_ref))
    pl.when(core == 1)(lambda: body(got_ref, kept_ref))


def pass_kernel(block_count, *refs):
    raw_refs, out_ref = refs[: len(RAW_MASKS)], refs[-1]
    power = raw_refs[0][:HALO, :]
    for ref in raw_refs[1:]:
        power = power + ref[:HALO, :]
    out_ref[:HALO, :] = power
    for number, ref in enumerate(raw_refs):
        out_ref[HALO + number * block_count : HALO + (number + 1) * block_count, :] = ref[HALO : HALO + block_count, :]


class Chip:
    def __init__(self, sizes, shifts_ref):
        self.subband_count, self.row_count, self.block_count = sizes
        self.shifts_ref = shifts_ref
        self.index = lax.axis_index("freq")
        self.core, self.chip, self.upper = self.index & 1, (self.index >> 1) & 7, self.index >> 4
        self.y, self.z, self.far = self.chip & 1, (self.chip >> 1) & 1, (self.chip >> 2) & 1

    def delays(self, level, group):
        bits = (self.core, self.y, self.z, self.far)
        node = self.subband_count - (self.subband_count >> level) + (self.upper << (3 - level)) + group
        column = bits[level] * self.row_count
        for above in range(level + 1, 4):
            column = column + (bits[above] << (4 + level - above))
        return delays_at(self.shifts_ref, node, 1, column, 2 << level)[0]


def chip_levels(sizes, shifts_ref, *refs):
    count = 1 + len(MERGED_MASKS)
    merged, raw, (passed_ref, first, second) = refs[:count], refs[count:-3], refs[-3:]
    here = Chip(sizes, shifts_ref)
    block_count = here.block_count
    power = passed_ref[:HALO, :]
    for number, (mask, ref) in enumerate(zip(RAW_MASKS, raw)):
        base = HALO + 2 * number * block_count
        own, other = here.core * block_count, (1 - here.core) * block_count
        second[lines_at(base + own, block_count), :] = ref[HALO + block_count :, :]
        at = HALO + number * block_count
        second[lines_at(base + other, block_count), :] = passed_ref[at : at + block_count, :]
        delays = here.delays(0, here.chip ^ mask)
        at = HALO + (here.chip ^ mask) * 2 * block_count
        merge(second, base, base + block_count, delays, first, at, block_count)
        power = power + ref[:HALO, :]
    for mask, ref in zip((0,) + MERGED_MASKS, merged):
        first[lines_at(HALO + (here.chip ^ mask) * 2 * block_count, 2 * block_count), :] = ref[HALO:, :]
        power = power + ref[:HALO, :]
    for level in range(1, 3):
        span = block_count << level
        for group in range(8 >> level):
            at = HALO + 2 * span * group
            merge(first, at, at + span, here.delays(level, group), second, at, block_count)
        first, second = second, first
    last = functools.partial(merge, first, HALO, HALO + 8 * block_count, here.delays(3, 0), second, HALO, block_count)
    return last, second, power


def packed_levels(sizes, low_bit, bit_count, shifts_ref, msg_ref, first, second):
    subband_count, row_count, block_count = sizes
    row_bits = row_count.bit_length() - 1
    index = lax.axis_index("freq")
    power = jnp.zeros((HALO, LANES), jnp.float32)
    span = (row_count >> bit_count) * block_count
    for message in range(1 << bit_count):
        at = HALO + reversed_bits(message, bit_count) * span
        start = message * (HALO + span)
        power = power + msg_ref[start : start + HALO, :]
        first[at : at + span, :] = msg_ref[start + HALO : start + HALO + span, :]
    own = [(index >> (low_bit + k)) & 1 for k in range(bit_count)]
    source, target = first, second
    for k in range(bit_count):
        level = low_bit + k
        span = (1 << (row_bits - bit_count + k)) * block_count
        column = own[k] * row_count
        for q in range(k + 1, bit_count):
            column = column + (own[q] << (row_bits - q + k))
        groups = 1 << (bit_count - k - 1)
        node = subband_count - (subband_count >> level) + ((index >> (low_bit + bit_count)) << (bit_count - k - 1))
        delays = delays_at(shifts_ref, node, groups, column, 2 * span // block_count)
        for group in range(groups):
            at = HALO + 2 * group * span
            last = functools.partial(merge, source, at, at + span, delays[group], target, at, block_count)
            if groups > 1:
                last()
        source, target = target, source
    return last, source, power


def merge_kernel(sizes, levels, next_bits, shifts_ref, *refs):
    msg_refs, (out_ref, first, second) = refs[:-3], refs[-3:]
    _, row_count, block_count = sizes
    last, final, power = levels(shifts_ref, *msg_refs, first, second)
    last()
    span = (row_count >> next_bits) * block_count
    for message in range(1 << next_bits):
        start = message * (HALO + span)
        out_ref[start : start + HALO, :] = power
        out_ref[start + HALO : start + HALO + span, :] = final[HALO + message * span : HALO + (message + 1) * span, :]


def table_kernel(prof_ref, after_ref, table_ref):
    prof_count, tap_count = prof_ref.shape
    span_len = table_ref.shape[1]
    profiles = jnp.concatenate(
        [prof_ref[...].astype(jnp.float32), jnp.zeros((prof_count, span_len - tap_count), jnp.float32)], axis=1
    )
    for offset in range(HOLD):
        moved = profiles if offset == 0 else pltpu.roll(profiles, offset * STRIDE, 1)
        table_ref[offset * prof_count : (offset + 1) * prof_count, :] = moved.astype(jnp.bfloat16)


def final_kernel(sizes, levels, shifts_ref, table_ref, *refs):
    msg_refs, (out_ref, first, second, windows) = refs[:-4], refs[-4:]
    subband_count, row_count, block_count = sizes
    prof_count = table_ref.shape[0] // HOLD
    last, final, power = levels(shifts_ref, *msg_refs, first, second)
    total = jnp.sum(jnp.sum(power, axis=0, keepdims=True), axis=1, keepdims=True)
    samples = subband_count * row_count * block_count * LANES
    rms_level = jnp.sqrt(subband_count * total / samples + 1e-06)
    line = lax.broadcasted_iota(jnp.int32, (block_count, LANES), 0)
    group = 256 // block_count
    for start in range(0, row_count, group):
        last(rows=range(start, start + group))
        for row in range(start, start + group):
            for block in range(table_ref.shape[1] // LANES):
                at = HALO + row * block_count + block
                piece = final[at : at + block_count, :]
                if block:
                    piece = jnp.where(line < block_count - block, piece, 0.0)
                windows[
                    row * block_count : (row + 1) * block_count, block * LANES : (block + 1) * LANES
                ] = piece.astype(jnp.bfloat16)
        products = lax.dot_general(
            table_ref[...],
            windows[start * block_count : (start + group) * block_count, :],
            (((1,), (1,)), ((), ())),
            preferred_element_type=jnp.float32,
        )
        best = products[:prof_count]
        for offset in range(1, HOLD):
            best = jnp.maximum(best, products[offset * prof_count : (offset + 1) * prof_count])
        best = best / rms_level
        for row in range(group):
            out_ref[start + row] = best[:, row * block_count : (row + 1) * block_count].astype(jnp.bfloat16)


def stage_groups(subband_count, low_bit, bit_count):
    groups = []
    for rest in range(subband_count >> bit_count):
        low = rest & ((1 << low_bit) - 1)
        high = rest >> low_bit
        groups.append(
            [
                low + (reversed_bits(slot, bit_count) << low_bit) + (high << (low_bit + bit_count))
                for slot in range(1 << bit_count)
            ]
        )
    return groups


def exchange(value, mask):
    return lax.ppermute(value, "freq", [(source, source ^ mask) for source in range(lax.axis_size("freq"))])


def call(kernel, out_shape, args, scratch=(), space=pltpu.VMEM):
    vmem = pl.BlockSpec(memory_space=pltpu.VMEM)
    return pl.pallas_call(
        kernel,
        out_shape=out_shape,
        in_specs=[pl.BlockSpec(memory_space=space)] * len(args),
        out_specs=jax.tree.map(lambda _: vmem, out_shape),
        scratch_shapes=list(scratch),
        compiler_params=pltpu.CompilerParams(vmem_limit_bytes=VMEM_LIMIT),
    )(*args)


def per_device(spectra, profiles, shifts):
    row_count, time_len = spectra.shape
    prof_count, tap_count = profiles.shape
    subband_count = lax.axis_size("freq")
    level_count = subband_count.bit_length() - 1
    row_bits = row_count.bit_length() - 1
    block_count = time_len // LANES
    sizes = (subband_count, row_count, block_count)
    stages = []
    while sum(stages) < level_count:
        stages.append(min(row_bits, level_count - sum(stages)))
    spectra = pltpu.with_memory_space_constraint(spectra, pltpu.HBM)
    states = [pltpu.VMEM((row_count * block_count + 2 * HALO, LANES), jnp.float32)] * 2
    fetch = [
        pltpu.VMEM(spectra.shape, jnp.float32),
        pltpu.SemaphoreType.DMA((FETCHES * row_count // 8,)),
    ]

    def lines(rows, tiles=1):
        return jax.ShapeDtypeStruct((rows * block_count + tiles * HALO, LANES), jnp.float32)

    def all_to_all(messages, low_bit, bit_count):
        shape = messages.shape
        pieces = messages.reshape(1 << bit_count, -1, LANES)
        groups = stage_groups(subband_count, low_bit, bit_count)
        return lax.all_to_all(pieces, "freq", 0, 0, tiled=True, axis_index_groups=groups).reshape(shape)

    if stages[0] == 4 and row_count == 16:
        half = row_count // 2
        *raw, sent, kept = call(
            split_kernel,
            [lines(2)] * len(RAW_MASKS) + [lines(half)] * 2,
            (spectra,),
            [pltpu.VMEM((row_count * (block_count + HALO), LANES), jnp.float32)] + fetch,
            pltpu.HBM,
        )
        raw = {mask: exchange(value, 2 * mask) for mask, value in zip(RAW_MASKS, raw)}
        got = exchange(sent, 1)
        own, *merged = call(
            functools.partial(core_merge_kernel, block_count, row_count),
            [lines(2)] * (1 + len(MERGED_MASKS)),
            (shifts, got, kept),
        )
        merged = {mask: exchange(value, 2 * mask) for mask, value in zip(MERGED_MASKS, merged)}
        passed = call(
            functools.partial(pass_kernel, block_count),
            lines(len(RAW_MASKS)),
            (*raw.values(), merged[PASS_AFTER]),
        )
        passed = exchange(passed, 1)
        after = own
        messages = [own, *merged.values(), *raw.values(), passed]
        levels = functools.partial(chip_levels, sizes)
    else:
        packed = call(pack_kernel, lines(row_count, 1 << stages[0]), (spectra,), fetch, pltpu.HBM)
        after = packed
        messages = [all_to_all(packed, 0, stages[0])]
        levels = functools.partial(packed_levels, sizes, 0, stages[0])
    low_bit = 0
    for bit_count, next_bits in zip(stages[:-1], stages[1:]):
        packed = call(
            functools.partial(merge_kernel, sizes, levels, next_bits),
            lines(row_count, 1 << next_bits),
            (shifts, *messages),
            states,
        )
        low_bit += bit_count
        messages = [all_to_all(packed, low_bit, next_bits)]
        levels = functools.partial(packed_levels, sizes, low_bit, next_bits)
    block_len = STRIDE * HOLD
    extra = (tap_count + block_len - STRIDE - 1) // block_len
    span_len = (extra + 1) * block_len
    table = call(table_kernel, jax.ShapeDtypeStruct((HOLD * prof_count, span_len), jnp.bfloat16), (profiles, after))
    return call(
        functools.partial(final_kernel, sizes, levels),
        jax.ShapeDtypeStruct((row_count, prof_count, block_count), jnp.bfloat16),
        (shifts, table, *messages),
        states + [pltpu.VMEM((row_count * block_count, span_len), jnp.bfloat16)],
    )


def solution(mesh):
    in_specs = (P(("beam", "freq"), None), P(), P())
    out_specs = P(("beam", "freq"), None, None)
    return jax.shard_map(
        per_device, mesh=mesh, in_specs=in_specs, out_specs=out_specs, check_vma=False
    )
```

time: 27 us -> 22.1 us (0.82)
  starting transfers between devices: 16.1 us -> 13.6 us
  waiting for transfers between devices: 4.85 us -> 3.44 us
  local copies, waits for them, and re-layouts: 1.05 us -> 0.01 us
    ppermute x10 -> x9, starting transfers between devices: 16.1 us -> 13.6 us  [exchange(): lax.ppermute(value, 'freq', [(source, source ^ mask) for source in range(...]
    ppermute x10 -> x9, waiting for transfers between devices: 4.85 us -> 3.44 us  [exchange(): lax.ppermute(value, 'freq', [(source, source ^ mask) for source in range(...]
    unnamed x6 -> x4, local copies, waits for them, and re-layouts: 1.05 us -> 0.01 us
    pallas_call x3 -> x5, Pallas kernels: 4.82 us -> 4.77 us  [call(): pl.pallas_call(kernel, out_shape=out_shape, in_specs=[pl.BlockSpec(memory...]
  transfers between devices with their start and end apart: 10 -> 9, of which waited for: 3 -> 3; matrix products, arithmetic and copies ran while one was open for 0% -> 0% of each run, Pallas kernels for 3% -> 2%
where the time goes in v3:
time: 22.1 us; the launch traced here: 21.9 us
  starting transfers between devices  13.6 us (62%)
  Pallas kernels  4.77 us (22%)
  waiting for transfers between devices  3.44 us (16%)
    ppermute x9, starting transfers between devices, exchange(): lax.ppermute(value, 'freq', [(source, source ^ mask) for source in range(...  13.6 us
    pallas_call x5, Pallas kernels, call(): pl.pallas_call(kernel, out_shape=out_shape, in_specs=[pl.BlockSpec(memory...  4.77 us
    ppermute x9, waiting for transfers between devices, exchange(): lax.ppermute(value, 'freq', [(source, source ^ mask) for source in range(...  3.44 us
  transfers between devices with their start and end apart: 9, of which 3 were waited for; matrix products, arithmetic and copies ran while one was open for 0% of the time, Pallas kernels for 2%

profile of v3, /device:TPU:0, one launch (start us, length us, event | category | flops | bytes accessed | tf_op | source)
XLA Modules:
  0.0 21.9 jit_solution(4478085893106250852)
XLA Ops:
  0.0 0.0 copy-start
  0.0 1.2 %shard_map.37 = (f32[136,128]{1,0:T(8,128)S(1)}, f32[136,128]{1,0:T(8,128)S(1)}, f32[520,128]{1,0:T(8,128)S(1)}, f32[520,128]{1,0:T(8,128)S(1)}) custom-call(f32[16,8192]{1,0:T(8,128)} %x_ref.1), custom_call_target="tpu_custom_call" | custom-call | tf_op jit(solution)/shard_map/pallas_call | solution.py:308
  1.2 0.5 %collective-permute-start = (f32[520,128]{1,0:T(8,128)S(1)}, f32[520,128]{1,0:T(8,128)S(1)}, u32[]{:S(2)}, u32[]{:S(2)}) collective-permute-start(f32[520,128]{1,0:T(8,128)S(1)} %get-tuple-element.15), channel_id=1, source_target_pairs={{0,1},{1,0},{2,3},{3,2},{4,5},{5,4},{6,7},{7,6},{8,9},{9,8},{10,11... | collective-permute-start | bytes 798728 | tf_op jit(solution)/shard_map/ppermute | solution.py:303
  1.7 5.6 %collective-permute-start.6 = (f32[136,128]{1,0:T(8,128)S(1)}, f32[136,128]{1,0:T(8,128)S(1)}, u32[]{:S(2)}, u32[]{:S(2)}) collective-permute-start(f32[136,128]{1,0:T(8,128)S(1)} %get-tuple-element.23), channel_id=1, source_target_pairs={{0,14},{1,15},{2,12},{3,13},{4,10},{5,11},{6,8},{7,9},{8,6},{9,7},... | collective-permute-start | bytes 208904 | tf_op jit(solution)/shard_map/ppermute | solution.py:303
  7.4 0.0 collective-permute-start.7
  7.4 0.0 collective-permute-done.got_ref
  7.4 0.0 copy-done
  7.4 0.3 %shard_map.38 = (f32[136,128]{1,0:T(8,128)S(1)}, f32[136,128]{1,0:T(8,128)S(1)}, f32[136,128]{1,0:T(8,128)S(1)}, f32[136,128]{1,0:T(8,128)S(1)}, f32[136,128]{1,0:T(8,128)S(1)}, /*index=5*/f32[136,128]{1,0:T(8,128)S(1)}) custom-call(s32[15,32]{1,0:T(8,128)S(1)} %copy-done, f32[520,128]{1,0:T(8,128)S(1)} %collective-permute-done.got_ref, ...), custom_call_target="tpu_custom_call" | custom-call | tf_op jit(solution)/shard_map/pallas_call | solution.py:308
  7.7 1.7 %collective-permute-start.3 = (f32[136,128]{1,0:T(8,128)S(1)}, f32[136,128]{1,0:T(8,128)S(1)}, u32[]{:S(2)}, u32[]{:S(2)}) collective-permute-start(f32[136,128]{1,0:T(8,128)S(1)} %get-tuple-element.20), channel_id=1, source_target_pairs={{0,6},{1,7},{2,4},{3,5},{4,2},{5,3},{6,0},{7,1},{8,14},{9,15},{10,... | collective-permute-start | bytes 208904 | tf_op jit(solution)/shard_map/ppermute | solution.py:303
  9.4 1.7 %collective-permute-start.1 = (f32[136,128]{1,0:T(8,128)S(1)}, f32[136,128]{1,0:T(8,128)S(1)}, u32[]{:S(2)}, u32[]{:S(2)}) collective-permute-start(f32[136,128]{1,0:T(8,128)S(1)} %get-tuple-element.18), channel_id=1, source_target_pairs={{0,8},{1,9},{2,10},{3,11},{4,12},{5,13},{6,14},{7,15},{8,0},{9,1},... | collective-permute-start | bytes 208904 | tf_op jit(solution)/shard_map/ppermute | solution.py:303
  11.1 1.9 %collective-permute-start.2 = (f32[136,128]{1,0:T(8,128)S(1)}, f32[136,128]{1,0:T(8,128)S(1)}, u32[]{:S(2)}, u32[]{:S(2)}) collective-permute-start(f32[136,128]{1,0:T(8,128)S(1)} %get-tuple-element.19), channel_id=1, source_target_pairs={{0,12},{1,13},{2,14},{3,15},{4,8},{5,9},{6,10},{7,11},{8,4},{9,5},... | collective-permute-start | bytes 208904 | tf_op jit(solution)/shard_map/ppermute | solution.py:303
  13.0 0.0 collective-permute-done.6.refs_0_.refs_6_
  13.0 0.6 %collective-permute-start.4 = (f32[136,128]{1,0:T(8,128)S(1)}, f32[136,128]{1,0:T(8,128)S(1)}, u32[]{:S(2)}, u32[]{:S(2)}) collective-permute-start(f32[136,128]{1,0:T(8,128)S(1)} %get-tuple-element.21), channel_id=1, source_target_pairs={{0,4},{1,5},{2,6},{3,7},{4,0},{5,1},{6,2},{7,3},{8,12},{9,13},{10,... | collective-permute-start | bytes 208904 | tf_op jit(solution)/shard_map/ppermute | solution.py:303
  13.6 0.7 %collective-permute-done.7.refs_1_.refs_7_ = f32[136,128]{1,0:T(8,128)S(1)} collective-permute-done((f32[136,128]{1,0:T(8,128)S(1)}, f32[136,128]{1,0:T(8,128)S(1)}, u32[]{:S(2)}, u32[]{:S(2)}) %collective-permute-start.7) | collective-permute-done | bytes 69664 | tf_op jit(solution)/shard_map/ppermute | solution.py:303
  14.3 0.0 copy-start.1
  14.3 1.5 %collective-permute-start.5 = (f32[136,128]{1,0:T(8,128)S(1)}, f32[136,128]{1,0:T(8,128)S(1)}, u32[]{:S(2)}, u32[]{:S(2)}) collective-permute-start(f32[136,128]{1,0:T(8,128)S(1)} %get-tuple-element.22), channel_id=1, source_target_pairs={{0,2},{1,3},{2,0},{3,1},{4,6},{5,7},{6,4},{7,5},{8,10},{9,11},{10,... | collective-permute-start | bytes 208904 | tf_op jit(solution)/shard_map/ppermute | solution.py:303
  15.8 0.0 collective-permute-done.3.refs_2_.refs_3_
  15.8 0.1 collective-permute-start.8
  15.9 0.0 copy-done.1
  15.9 0.2 shard_map.39.table_ref
  16.1 2.6 %collective-permute-done.1.refs_1_ = f32[136,128]{1,0:T(8,128)S(1)} collective-permute-done((f32[136,128]{1,0:T(8,128)S(1)}, f32[136,128]{1,0:T(8,128)S(1)}, u32[]{:S(2)}, u32[]{:S(2)}) %collective-permute-start.1) | collective-permute-done | bytes 69664 | tf_op jit(solution)/shard_map/ppermute | solution.py:303
  18.8 0.0 collective-permute-done.2.refs_2_
  18.8 0.1 collective-permute-done.4.refs_4_
  18.8 0.0 collective-permute-done.5.refs_5_
  18.8 0.0 collective-permute-done.8.refs_8_
  18.8 3.0 %shard_map.41 = bf16[16,64,64]{2,1,0:T(8,128)(2,1)} custom-call(s32[15,32]{1,0:T(8,128)S(1)} %copy-done, bf16[1024,384]{1,0:T(8,128)(2,1)S(1)} %shard_map.39.table_ref, f32[136,128]{1,0:T(8,128)S(1)} %get-tuple-element.17.after_ref.refs_0_, f32[136,128]{1,0:T(8,128)S(1)} %collective-permute-done.1.refs_1_, f32[136,128]{1,0:T(8,128)S(1)} %collective-permute-done.2.refs_2_, ...), custom_call_target="tpu_custom_call" | custom-call | tf_op jit(solution)/shard_map/pallas_call | solution.py:308
  (1 shorter events, 0.0 us)
Async XLA Ops:
  0.0 7.4 %copy-start = (s32[15,32]{1,0:T(8,128)S(1)}, s32[15,32]{1,0:T(8,128)}, u32[]{:S(2)}) copy-start(s32[15,32]{1,0:T(8,128)} %shifts_ref.3) | copy-start | bytes 5764
  1.2 6.2 %collective-permute-start = (f32[520,128]{1,0:T(8,128)S(1)}, f32[520,128]{1,0:T(8,128)S(1)}, u32[]{:S(2)}, u32[]{:S(2)}) collective-permute-start(f32[520,128]{1,0:T(8,128)S(1)} %get-tuple-element.15), channel_id=1, source_target_pairs={{0,1},{1,0},{2,3},{3,2},{4,5},{5,4},{6,7},{7,6},{8,9},{9,8},{10,11... | collective-permute-start | bytes 798728 | tf_op jit(solution)/shard_map/ppermute | solution.py:303
  1.7 11.3 %collective-permute-start.6 = (f32[136,128]{1,0:T(8,128)S(1)}, f32[136,128]{1,0:T(8,128)S(1)}, u32[]{:S(2)}, u32[]{:S(2)}) collective-permute-start(f32[136,128]{1,0:T(8,128)S(1)} %get-tuple-element.23), channel_id=1, source_target_pairs={{0,14},{1,15},{2,12},{3,13},{4,10},{5,11},{6,8},{7,9},{8,6},{9,7},... | collective-permute-start | bytes 208904 | tf_op jit(solution)/shard_map/ppermute | solution.py:303
  7.4 7.0 %collective-permute-start.7 = (f32[136,128]{1,0:T(8,128)S(1)}, f32[136,128]{1,0:T(8,128)S(1)}, u32[]{:S(2)}, u32[]{:S(2)}) collective-permute-start(f32[136,128]{1,0:T(8,128)S(1)} %get-tuple-element.24), channel_id=1, source_target_pairs={{0,10},{1,11},{2,8},{3,9},{4,14},{5,15},{6,12},{7,13},{8,2},{9,3},... | collective-permute-start | bytes 208904 | tf_op jit(solution)/shard_map/ppermute | solution.py:303
  7.7 8.1 %collective-permute-start.3 = (f32[136,128]{1,0:T(8,128)S(1)}, f32[136,128]{1,0:T(8,128)S(1)}, u32[]{:S(2)}, u32[]{:S(2)}) collective-permute-start(f32[136,128]{1,0:T(8,128)S(1)} %get-tuple-element.20), channel_id=1, source_target_pairs={{0,6},{1,7},{2,4},{3,5},{4,2},{5,3},{6,0},{7,1},{8,14},{9,15},{10,... | collective-permute-start | bytes 208904 | tf_op jit(solution)/shard_map/ppermute | solution.py:303
  9.4 9.3 %collective-permute-start.1 = (f32[136,128]{1,0:T(8,128)S(1)}, f32[136,128]{1,0:T(8,128)S(1)}, u32[]{:S(2)}, u32[]{:S(2)}) collective-permute-start(f32[136,128]{1,0:T(8,128)S(1)} %get-tuple-element.18), channel_id=1, source_target_pairs={{0,8},{1,9},{2,10},{3,11},{4,12},{5,13},{6,14},{7,15},{8,0},{9,1},... | collective-permute-start | bytes 208904 | tf_op jit(solution)/shard_map/ppermute | solution.py:303
  11.1 7.7 %collective-permute-start.2 = (f32[136,128]{1,0:T(8,128)S(1)}, f32[136,128]{1,0:T(8,128)S(1)}, u32[]{:S(2)}, u32[]{:S(2)}) collective-permute-start(f32[136,128]{1,0:T(8,128)S(1)} %get-tuple-element.19), channel_id=1, source_target_pairs={{0,12},{1,13},{2,14},{3,15},{4,8},{5,9},{6,10},{7,11},{8,4},{9,5},... | collective-permute-start | bytes 208904 | tf_op jit(solution)/shard_map/ppermute | solution.py:303
  13.0 5.8 %collective-permute-start.4 = (f32[136,128]{1,0:T(8,128)S(1)}, f32[136,128]{1,0:T(8,128)S(1)}, u32[]{:S(2)}, u32[]{:S(2)}) collective-permute-start(f32[136,128]{1,0:T(8,128)S(1)} %get-tuple-element.21), channel_id=1, source_target_pairs={{0,4},{1,5},{2,6},{3,7},{4,0},{5,1},{6,2},{7,3},{8,12},{9,13},{10,... | collective-permute-start | bytes 208904 | tf_op jit(solution)/shard_map/ppermute | solution.py:303
  14.3 1.6 %copy-start.1 = (bf16[64,256]{1,0:T(8,128)(2,1)S(1)}, bf16[64,256]{1,0:T(8,128)(2,1)}, u32[]{:S(2)}) copy-start(bf16[64,256]{1,0:T(8,128)(2,1)} %prof_ref.1) | copy-start | bytes 98308
  14.3 4.5 %collective-permute-start.5 = (f32[136,128]{1,0:T(8,128)S(1)}, f32[136,128]{1,0:T(8,128)S(1)}, u32[]{:S(2)}, u32[]{:S(2)}) collective-permute-start(f32[136,128]{1,0:T(8,128)S(1)} %get-tuple-element.22), channel_id=1, source_target_pairs={{0,2},{1,3},{2,0},{3,1},{4,6},{5,7},{6,4},{7,5},{8,10},{9,11},{10,... | collective-permute-start | bytes 208904 | tf_op jit(solution)/shard_map/ppermute | solution.py:303
  15.8 3.0 %collective-permute-start.8 = (f32[136,128]{1,0:T(8,128)S(1)}, f32[136,128]{1,0:T(8,128)S(1)}, u32[]{:S(2)}, u32[]{:S(2)}) collective-permute-start(f32[136,128]{1,0:T(8,128)S(1)} %shard_map.40), channel_id=1, source_target_pairs={{0,1},{1,0},{2,3},{3,2},{4,5},{5,4},{6,7},{7,6},{8,9},{9,8},{10,11... | collective-permute-start | bytes 208904 | tf_op jit(solution)/shard_map/ppermute | solution.py:303

commit v4 on v3

--- a/solution.py
+++ b/solution.py
@@ -11,6 +11,7 @@
 HOLD = 16
 LANES = 128
 HALO = 8
+GROUP = 256
 VMEM_LIMIT = 48 * 1024 * 1024
 FETCHES = 4
 RAW_MASKS = (7, 5)
@@ -26,6 +27,8 @@
 
 
 def lines_at(start, count):
+    if isinstance(start, int):
+        return slice(start, start + count)
     return pl.ds(pl.multiple_of(start, 8), count)
 
 
@@ -64,30 +67,29 @@
 
 
 def split_kernel(x_ref, *refs):
-    raw_refs, (sent_ref, kept_ref, rows, buffer, sems) = refs[:-5], refs[-5:]
+    raw_refs, (sent_ref, kept_ref, buffer, sems) = refs[:-4], refs[-4:]
     index = lax.axis_index("freq")
     core, chip = index & 1, (index >> 1) & 7
     row_count, time_len = x_ref.shape
     block_count = time_len // LANES
-    half_rows = row_count // 2
     stride = block_count + HALO
 
-    def store(half, column, piece):
-        rows[pl.ds(half * 8 * stride + column, 8, stride=stride), :] = piece
-
-    power = aligned_rows(x_ref, buffer, sems, store)
-    for ref in (*raw_refs, sent_ref, kept_ref):
-        ref[:HALO, :] = power
-    sent_at, kept_at = (1 - core) * half_rows * stride, core * half_rows * stride
-    for mask, out_ref in zip(RAW_MASKS, raw_refs):
-        at = reversed_bits(chip ^ mask, 3) * stride
-        out_ref[HALO : HALO + block_count, :] = rows[lines_at(sent_at + at, block_count), :]
-        out_ref[HALO + block_count :, :] = rows[lines_at(kept_at + at, block_count), :]
-    for row in range(half_rows):
-        for ref, at in ((sent_ref, sent_at), (kept_ref, kept_at)):
-            ref[HALO + row * block_count : HALO + (row + 1) * block_count, :] = rows[
-                lines_at(at + row * stride, block_count), :
-            ]
+    def body(own_half):
+        def store(half, column, piece):
+            ref = kept_ref if half == own_half else sent_ref
+            ref[pl.ds(HALO + column, 8, stride=stride), :] = piece
+
+        power = aligned_rows(x_ref, buffer, sems, store)
+        for mask, out_ref in zip(RAW_MASKS, raw_refs):
+            at = HALO + reversed_bits(chip ^ mask, 3) * stride
+            out_ref[:HALO, :] = power
+            out_ref[HALO : HALO + block_count, :] = sent_ref[lines_at(at, block_count), :]
+            out_ref[HALO + block_count :, :] = kept_ref[lines_at(at, block_count), :]
+        for ref in (sent_ref, kept_ref):
+            ref[:HALO, :] = power
+
+    for own_half in range(2):
+        pl.when(core == own_half)(functools.partial(body, own_half))
 
 
 def delays_at(shifts_ref, node, groups, column, count):
@@ -128,7 +130,7 @@
     def body(low_ref, high_ref):
         power = low_ref[:HALO, :] + high_ref[:HALO, :]
         for mask, out_ref in zip((0,) + MERGED_MASKS, outs):
-            at = HALO + reversed_bits(chip ^ mask, 3) * block_count
+            at = HALO + reversed_bits(chip ^ mask, 3) * (block_count + HALO)
             for part in range(2):
                 delay = picked[2 * reversed_bits(mask, 3) + part, 0]
                 out_ref[HALO + part * block_count : HALO + (part + 1) * block_count, :] = low_ref[
@@ -192,8 +194,7 @@
             at = HALO + 2 * span * group
             merge(first, at, at + span, here.delays(level, group), second, at, block_count)
         first, second = second, first
-    last = functools.partial(merge, first, HALO, HALO + 8 * block_count, here.delays(3, 0), second, HALO, block_count)
-    return last, second, power
+    return functools.partial(merge, first, HALO, HALO + 8 * block_count, here.delays(3, 0)), power
 
 
 def packed_levels(sizes, low_bit, bit_count, shifts_ref, msg_ref, first, second):
@@ -220,18 +221,18 @@
         delays = delays_at(shifts_ref, node, groups, column, 2 * span // block_count)
         for group in range(groups):
             at = HALO + 2 * group * span
-            last = functools.partial(merge, source, at, at + span, delays[group], target, at, block_count)
+            last = functools.partial(merge, source, at, at + span, delays[group])
             if groups > 1:
-                last()
+                last(target, at, block_count)
         source, target = target, source
-    return last, source, power
+    return last, power
 
 
 def merge_kernel(sizes, levels, next_bits, shifts_ref, *refs):
-    msg_refs, (out_ref, first, second) = refs[:-3], refs[-3:]
+    msg_refs, (out_ref, first, second, final) = refs[:-4], refs[-4:]
     _, row_count, block_count = sizes
-    last, final, power = levels(shifts_ref, *msg_refs, first, second)
-    last()
+    last, power = levels(shifts_ref, *msg_refs, first, second)
+    last(final, HALO, block_count)
     span = (row_count >> next_bits) * block_count
     for message in range(1 << next_bits):
         start = message * (HALO + span)
@@ -251,18 +252,23 @@
 
 
 def final_kernel(sizes, levels, shifts_ref, table_ref, *refs):
-    msg_refs, (out_ref, first, second, windows) = refs[:-4], refs[-4:]
+    groups = sizes[1] * sizes[2] // GROUP
+    scratch = refs[-2 * groups :]
+    msg_refs, (out_ref, first, second) = refs[: -3 - 2 * groups], refs[-3 - 2 * groups : -2 * groups]
     subband_count, row_count, block_count = sizes
     prof_count = table_ref.shape[0] // HOLD
-    last, final, power = levels(shifts_ref, *msg_refs, first, second)
+    last, power = levels(shifts_ref, *msg_refs, first, second)
     total = jnp.sum(jnp.sum(power, axis=0, keepdims=True), axis=1, keepdims=True)
     samples = subband_count * row_count * block_count * LANES
     rms_level = jnp.sqrt(subband_count * total / samples + 1e-06)
     line = lax.broadcasted_iota(jnp.int32, (block_count, LANES), 0)
-    group = 256 // block_count
-    for start in range(0, row_count, group):
-        last(rows=range(start, start + group))
-        for row in range(start, start + group):
+    group = GROUP // block_count
+
+    def window(number):
+        final, windows = scratch[2 * number : 2 * number + 2]
+        rows = range(number * group, (number + 1) * group)
+        last(final, HALO - rows[0] * block_count, block_count, rows)
+        for row in range(group):
             for block in range(table_ref.shape[1] // LANES):
                 at = HALO + row * block_count + block
                 piece = final[at : at + block_count, :]
@@ -271,9 +277,14 @@
                 windows[
                     row * block_count : (row + 1) * block_count, block * LANES : (block + 1) * LANES
                 ] = piece.astype(jnp.bfloat16)
+
+    window(0)
+    for number in range(groups):
+        if number + 1 < groups:
+            window(number + 1)
         products = lax.dot_general(
             table_ref[...],
-            windows[start * block_count : (start + group) * block_count, :],
+            scratch[2 * number + 1][...],
             (((1,), (1,)), ((), ())),
             preferred_element_type=jnp.float32,
         )
@@ -282,7 +293,7 @@
             best = jnp.maximum(best, products[offset * prof_count : (offset + 1) * prof_count])
         best = best / rms_level
         for row in range(group):
-            out_ref[start + row] = best[:, row * block_count : (row + 1) * block_count].astype(jnp.bfloat16)
+            out_ref[number * group + row] = best[:, row * block_count : (row + 1) * block_count].astype(jnp.bfloat16)
 
 
 def stage_groups(subband_count, low_bit, bit_count):
@@ -346,9 +357,9 @@
         half = row_count // 2
         *raw, sent, kept = call(
             split_kernel,
-            [lines(2)] * len(RAW_MASKS) + [lines(half)] * 2,
+            [lines(2)] * len(RAW_MASKS) + [lines(half, half + 1)] * 2,
             (spectra,),
-            [pltpu.VMEM((row_count * (block_count + HALO), LANES), jnp.float32)] + fetch,
+            fetch,
             pltpu.HBM,
         )
         raw = {mask: exchange(value, 2 * mask) for mask, value in zip(RAW_MASKS, raw)}
@@ -379,7 +390,7 @@
             functools.partial(merge_kernel, sizes, levels, next_bits),
             lines(row_count, 1 << next_bits),
             (shifts, *messages),
-            states,
+            states + states[:1],
         )
         low_bit += bit_count
         messages = [all_to_all(packed, low_bit, next_bits)]
@@ -392,7 +403,12 @@
         functools.partial(final_kernel, sizes, levels),
         jax.ShapeDtypeStruct((row_count, prof_count, block_count), jnp.bfloat16),
         (shifts, table, *messages),
-        states + [pltpu.VMEM((row_count * block_count, span_len), jnp.bfloat16)],
+        states
+        + [
+            pltpu.VMEM((GROUP + 2 * HALO, LANES), jnp.float32),
+            pltpu.VMEM((GROUP, span_len), jnp.bfloat16),
+        ]
+        * (row_count * block_count // GROUP),
     )
 
 

time: 22.1 us -> 22.1 us (level)
  no operation moved by 1% of the time
where the time goes in v4:
time: 22.1 us; the launch traced here: 21.9 us
  starting transfers between devices  13.6 us (62%)
  Pallas kernels  4.75 us (21%)
  waiting for transfers between devices  3.44 us (16%)
    ppermute x9, starting transfers between devices, exchange(): lax.ppermute(value, 'freq', [(source, source ^ mask) for source in range(...  13.6 us
    pallas_call x5, Pallas kernels, call(): pl.pallas_call(kernel, out_shape=out_shape, in_specs=[pl.BlockSpec(memory...  4.75 us
    ppermute x9, waiting for transfers between devices, exchange(): lax.ppermute(value, 'freq', [(source, source ^ mask) for source in range(...  3.44 us
  transfers between devices with their start and end apart: 9, of which 3 were waited for; matrix products, arithmetic and copies ran while one was open for 0% of the time, Pallas kernels for 2%

profile of v4, /device:TPU:0, one launch (start us, length us, event | category | flops | bytes accessed | tf_op | source)
XLA Modules:
  0.0 21.9 jit_solution(8037794697601201702)
XLA Ops:
  0.0 0.0 copy-start
  0.0 1.2 %shard_map.37 = (f32[136,128]{1,0:T(8,128)S(1)}, f32[136,128]{1,0:T(8,128)S(1)}, f32[584,128]{1,0:T(8,128)S(1)}, f32[584,128]{1,0:T(8,128)S(1)}) custom-call(f32[16,8192]{1,0:T(8,128)} %x_ref.1), custom_call_target="tpu_custom_call" | custom-call | tf_op jit(solution)/shard_map/pallas_call | solution.py:319
  1.2 0.5 %collective-permute-start = (f32[584,128]{1,0:T(8,128)S(1)}, f32[584,128]{1,0:T(8,128)S(1)}, u32[]{:S(2)}, u32[]{:S(2)}) collective-permute-start(f32[584,128]{1,0:T(8,128)S(1)} %get-tuple-element.15), channel_id=1, source_target_pairs={{0,1},{1,0},{2,3},{3,2},{4,5},{5,4},{6,7},{7,6},{8,9},{9,8},{10,11... | collective-permute-start | bytes 897032 | tf_op jit(solution)/shard_map/ppermute | solution.py:314
  1.7 5.6 %collective-permute-start.6 = (f32[136,128]{1,0:T(8,128)S(1)}, f32[136,128]{1,0:T(8,128)S(1)}, u32[]{:S(2)}, u32[]{:S(2)}) collective-permute-start(f32[136,128]{1,0:T(8,128)S(1)} %get-tuple-element.23), channel_id=1, source_target_pairs={{0,14},{1,15},{2,12},{3,13},{4,10},{5,11},{6,8},{7,9},{8,6},{9,7},... | collective-permute-start | bytes 208904 | tf_op jit(solution)/shard_map/ppermute | solution.py:314
  7.3 0.0 collective-permute-start.7
  7.3 0.0 collective-permute-done.got_ref
  7.3 0.0 copy-done
  7.3 0.3 %shard_map.38 = (f32[136,128]{1,0:T(8,128)S(1)}, f32[136,128]{1,0:T(8,128)S(1)}, f32[136,128]{1,0:T(8,128)S(1)}, f32[136,128]{1,0:T(8,128)S(1)}, f32[136,128]{1,0:T(8,128)S(1)}, /*index=5*/f32[136,128]{1,0:T(8,128)S(1)}) custom-call(s32[15,32]{1,0:T(8,128)S(1)} %copy-done, f32[584,128]{1,0:T(8,128)S(1)} %collective-permute-done.got_ref, ...), custom_call_target="tpu_custom_call" | custom-call | tf_op jit(solution)/shard_map/pallas_call | solution.py:319
  7.7 1.7 %collective-permute-start.3 = (f32[136,128]{1,0:T(8,128)S(1)}, f32[136,128]{1,0:T(8,128)S(1)}, u32[]{:S(2)}, u32[]{:S(2)}) collective-permute-start(f32[136,128]{1,0:T(8,128)S(1)} %get-tuple-element.20), channel_id=1, source_target_pairs={{0,6},{1,7},{2,4},{3,5},{4,2},{5,3},{6,0},{7,1},{8,14},{9,15},{10,... | collective-permute-start | bytes 208904 | tf_op jit(solution)/shard_map/ppermute | solution.py:314
  9.4 1.7 %collective-permute-start.1 = (f32[136,128]{1,0:T(8,128)S(1)}, f32[136,128]{1,0:T(8,128)S(1)}, u32[]{:S(2)}, u32[]{:S(2)}) collective-permute-start(f32[136,128]{1,0:T(8,128)S(1)} %get-tuple-element.18), channel_id=1, source_target_pairs={{0,8},{1,9},{2,10},{3,11},{4,12},{5,13},{6,14},{7,15},{8,0},{9,1},... | collective-permute-start | bytes 208904 | tf_op jit(solution)/shard_map/ppermute | solution.py:314
  11.1 1.9 %collective-permute-start.2 = (f32[136,128]{1,0:T(8,128)S(1)}, f32[136,128]{1,0:T(8,128)S(1)}, u32[]{:S(2)}, u32[]{:S(2)}) collective-permute-start(f32[136,128]{1,0:T(8,128)S(1)} %get-tuple-element.19), channel_id=1, source_target_pairs={{0,12},{1,13},{2,14},{3,15},{4,8},{5,9},{6,10},{7,11},{8,4},{9,5},... | collective-permute-start | bytes 208904 | tf_op jit(solution)/shard_map/ppermute | solution.py:314
  13.0 0.0 collective-permute-done.6.refs_0_.refs_6_
  13.0 0.6 %collective-permute-start.4 = (f32[136,128]{1,0:T(8,128)S(1)}, f32[136,128]{1,0:T(8,128)S(1)}, u32[]{:S(2)}, u32[]{:S(2)}) collective-permute-start(f32[136,128]{1,0:T(8,128)S(1)} %get-tuple-element.21), channel_id=1, source_target_pairs={{0,4},{1,5},{2,6},{3,7},{4,0},{5,1},{6,2},{7,3},{8,12},{9,13},{10,... | collective-permute-start | bytes 208904 | tf_op jit(solution)/shard_map/ppermute | solution.py:314
  13.6 0.7 %collective-permute-done.7.refs_1_.refs_7_ = f32[136,128]{1,0:T(8,128)S(1)} collective-permute-done((f32[136,128]{1,0:T(8,128)S(1)}, f32[136,128]{1,0:T(8,128)S(1)}, u32[]{:S(2)}, u32[]{:S(2)}) %collective-permute-start.7) | collective-permute-done | bytes 69664 | tf_op jit(solution)/shard_map/ppermute | solution.py:314
  14.3 0.0 copy-start.1
  14.3 1.5 %collective-permute-start.5 = (f32[136,128]{1,0:T(8,128)S(1)}, f32[136,128]{1,0:T(8,128)S(1)}, u32[]{:S(2)}, u32[]{:S(2)}) collective-permute-start(f32[136,128]{1,0:T(8,128)S(1)} %get-tuple-element.22), channel_id=1, source_target_pairs={{0,2},{1,3},{2,0},{3,1},{4,6},{5,7},{6,4},{7,5},{8,10},{9,11},{10,... | collective-permute-start | bytes 208904 | tf_op jit(solution)/shard_map/ppermute | solution.py:314
  15.8 0.0 collective-permute-done.3.refs_2_.refs_3_
  15.8 0.1 collective-permute-start.8
  15.9 0.0 copy-done.1
  15.9 0.2 shard_map.39.table_ref
  16.1 2.6 %collective-permute-done.1.refs_1_ = f32[136,128]{1,0:T(8,128)S(1)} collective-permute-done((f32[136,128]{1,0:T(8,128)S(1)}, f32[136,128]{1,0:T(8,128)S(1)}, u32[]{:S(2)}, u32[]{:S(2)}) %collective-permute-start.1) | collective-permute-done | bytes 69664 | tf_op jit(solution)/shard_map/ppermute | solution.py:314
  18.7 0.0 collective-permute-done.2.refs_2_
  18.7 0.1 collective-permute-done.4.refs_4_
  18.8 0.0 collective-permute-done.5.refs_5_
  18.8 0.0 collective-permute-done.8.refs_8_
  18.8 3.0 %shard_map.41 = bf16[16,64,64]{2,1,0:T(8,128)(2,1)} custom-call(s32[15,32]{1,0:T(8,128)S(1)} %copy-done, bf16[1024,384]{1,0:T(8,128)(2,1)S(1)} %shard_map.39.table_ref, f32[136,128]{1,0:T(8,128)S(1)} %get-tuple-element.17.after_ref.refs_0_, f32[136,128]{1,0:T(8,128)S(1)} %collective-permute-done.1.refs_1_, f32[136,128]{1,0:T(8,128)S(1)} %collective-permute-done.2.refs_2_, ...), custom_call_target="tpu_custom_call" | custom-call | tf_op jit(solution)/shard_map/pallas_call | solution.py:319
  (1 shorter events, 0.0 us)
Async XLA Ops:
  0.0 7.3 %copy-start = (s32[15,32]{1,0:T(8,128)S(1)}, s32[15,32]{1,0:T(8,128)}, u32[]{:S(2)}) copy-start(s32[15,32]{1,0:T(8,128)} %shifts_ref.3) | copy-start | bytes 5764
  1.2 6.2 %collective-permute-start = (f32[584,128]{1,0:T(8,128)S(1)}, f32[584,128]{1,0:T(8,128)S(1)}, u32[]{:S(2)}, u32[]{:S(2)}) collective-permute-start(f32[584,128]{1,0:T(8,128)S(1)} %get-tuple-element.15), channel_id=1, source_target_pairs={{0,1},{1,0},{2,3},{3,2},{4,5},{5,4},{6,7},{7,6},{8,9},{9,8},{10,11... | collective-permute-start | bytes 897032 | tf_op jit(solution)/shard_map/ppermute | solution.py:314
  1.7 11.3 %collective-permute-start.6 = (f32[136,128]{1,0:T(8,128)S(1)}, f32[136,128]{1,0:T(8,128)S(1)}, u32[]{:S(2)}, u32[]{:S(2)}) collective-permute-start(f32[136,128]{1,0:T(8,128)S(1)} %get-tuple-element.23), channel_id=1, source_target_pairs={{0,14},{1,15},{2,12},{3,13},{4,10},{5,11},{6,8},{7,9},{8,6},{9,7},... | collective-permute-start | bytes 208904 | tf_op jit(solution)/shard_map/ppermute | solution.py:314
  7.3 7.0 %collective-permute-start.7 = (f32[136,128]{1,0:T(8,128)S(1)}, f32[136,128]{1,0:T(8,128)S(1)}, u32[]{:S(2)}, u32[]{:S(2)}) collective-permute-start(f32[136,128]{1,0:T(8,128)S(1)} %get-tuple-element.24), channel_id=1, source_target_pairs={{0,10},{1,11},{2,8},{3,9},{4,14},{5,15},{6,12},{7,13},{8,2},{9,3},... | collective-permute-start | bytes 208904 | tf_op jit(solution)/shard_map/ppermute | solution.py:314
  7.7 8.1 %collective-permute-start.3 = (f32[136,128]{1,0:T(8,128)S(1)}, f32[136,128]{1,0:T(8,128)S(1)}, u32[]{:S(2)}, u32[]{:S(2)}) collective-permute-start(f32[136,128]{1,0:T(8,128)S(1)} %get-tuple-element.20), channel_id=1, source_target_pairs={{0,6},{1,7},{2,4},{3,5},{4,2},{5,3},{6,0},{7,1},{8,14},{9,15},{10,... | collective-permute-start | bytes 208904 | tf_op jit(solution)/shard_map/ppermute | solution.py:314
  9.4 9.3 %collective-permute-start.1 = (f32[136,128]{1,0:T(8,128)S(1)}, f32[136,128]{1,0:T(8,128)S(1)}, u32[]{:S(2)}, u32[]{:S(2)}) collective-permute-start(f32[136,128]{1,0:T(8,128)S(1)} %get-tuple-element.18), channel_id=1, source_target_pairs={{0,8},{1,9},{2,10},{3,11},{4,12},{5,13},{6,14},{7,15},{8,0},{9,1},... | collective-permute-start | bytes 208904 | tf_op jit(solution)/shard_map/ppermute | solution.py:314
  11.1 7.7 %collective-permute-start.2 = (f32[136,128]{1,0:T(8,128)S(1)}, f32[136,128]{1,0:T(8,128)S(1)}, u32[]{:S(2)}, u32[]{:S(2)}) collective-permute-start(f32[136,128]{1,0:T(8,128)S(1)} %get-tuple-element.19), channel_id=1, source_target_pairs={{0,12},{1,13},{2,14},{3,15},{4,8},{5,9},{6,10},{7,11},{8,4},{9,5},... | collective-permute-start | bytes 208904 | tf_op jit(solution)/shard_map/ppermute | solution.py:314
  13.0 5.8 %collective-permute-start.4 = (f32[136,128]{1,0:T(8,128)S(1)}, f32[136,128]{1,0:T(8,128)S(1)}, u32[]{:S(2)}, u32[]{:S(2)}) collective-permute-start(f32[136,128]{1,0:T(8,128)S(1)} %get-tuple-element.21), channel_id=1, source_target_pairs={{0,4},{1,5},{2,6},{3,7},{4,0},{5,1},{6,2},{7,3},{8,12},{9,13},{10,... | collective-permute-start | bytes 208904 | tf_op jit(solution)/shard_map/ppermute | solution.py:314
  14.3 1.6 %copy-start.1 = (bf16[64,256]{1,0:T(8,128)(2,1)S(1)}, bf16[64,256]{1,0:T(8,128)(2,1)}, u32[]{:S(2)}) copy-start(bf16[64,256]{1,0:T(8,128)(2,1)} %prof_ref.1) | copy-start | bytes 98308
  14.3 4.5 %collective-permute-start.5 = (f32[136,128]{1,0:T(8,128)S(1)}, f32[136,128]{1,0:T(8,128)S(1)}, u32[]{:S(2)}, u32[]{:S(2)}) collective-permute-start(f32[136,128]{1,0:T(8,128)S(1)} %get-tuple-element.22), channel_id=1, source_target_pairs={{0,2},{1,3},{2,0},{3,1},{4,6},{5,7},{6,4},{7,5},{8,10},{9,11},{10,... | collective-permute-start | bytes 208904 | tf_op jit(solution)/shard_map/ppermute | solution.py:314
  15.8 3.0 %collective-permute-start.8 = (f32[136,128]{1,0:T(8,128)S(1)}, f32[136,128]{1,0:T(8,128)S(1)}, u32[]{:S(2)}, u32[]{:S(2)}) collective-permute-start(f32[136,128]{1,0:T(8,128)S(1)} %shard_map.40), channel_id=1, source_target_pairs={{0,1},{1,0},{2,3},{3,2},{4,5},{5,4},{6,7},{7,6},{8,9},{9,8},{10,11... | collective-permute-start | bytes 208904 | tf_op jit(solution)/shard_map/ppermute | solution.py:314

commit v5 on v4

--- a/solution.py
+++ b/solution.py
@@ -15,7 +15,10 @@
 VMEM_LIMIT = 48 * 1024 * 1024
 FETCHES = 4
 RAW_MASKS = (7, 5)
-MERGED_MASKS = (4, 6, 3, 2, 1)
+NEAR_LINES = 7
+FAR_MASKS = (4, 6)
+NEAR_MASKS = (3, 2, 1)
+MERGED_MASKS = FAR_MASKS + NEAR_MASKS
 PASS_AFTER = 3
 
 
@@ -133,10 +136,14 @@
             at = HALO + reversed_bits(chip ^ mask, 3) * (block_count + HALO)
             for part in range(2):
                 delay = picked[2 * reversed_bits(mask, 3) + part, 0]
-                out_ref[HALO + part * block_count : HALO + (part + 1) * block_count, :] = low_ref[
-                    lines_at(at, block_count), :
-                ] + delayed(high_ref, at, delay, block_count)
-            out_ref[:HALO, :] = power
+                start = part * block_count + (HALO if mask in FAR_MASKS else 0)
+                out_ref[start : start + block_count, :] = low_ref[lines_at(at, block_count), :] + delayed(
+                    high_ref, at, delay, block_count
+                )
+            if mask in FAR_MASKS:
+                out_ref[:HALO, :] = power
+            else:
+                out_ref[2 * block_count :, :] = jnp.broadcast_to(jnp.sum(power, axis=0, keepdims=True), (NEAR_LINES, LANES))
 
     pl.when(core == 0)(lambda: body(kept_ref, got_ref))
     pl.when(core == 1)(lambda: body(got_ref, kept_ref))
@@ -147,9 +154,10 @@
     power = raw_refs[0][:HALO, :]
     for ref in raw_refs[1:]:
         power = power + ref[:HALO, :]
-    out_ref[:HALO, :] = power
     for number, ref in enumerate(raw_refs):
-        out_ref[HALO + number * block_count : HALO + (number + 1) * block_count, :] = ref[HALO : HALO + block_count, :]
+        out_ref[number * block_count : (number + 1) * block_count, :] = ref[HALO : HALO + block_count, :]
+    end = len(raw_refs) * block_count
+    out_ref[end:, :] = jnp.broadcast_to(jnp.sum(power, axis=0, keepdims=True), (NEAR_LINES, LANES))
 
 
 class Chip:
@@ -169,32 +177,52 @@
         return delays_at(self.shifts_ref, node, 1, column, 2 << level)[0]
 
 
-def chip_levels(sizes, shifts_ref, *refs):
-    count = 1 + len(MERGED_MASKS)
-    merged, raw, (passed_ref, first, second) = refs[:count], refs[count:-3], refs[-3:]
+def near_kernel(sizes, shifts_ref, *refs):
+    near, (out_ref, first, second) = refs[:4], refs[4:]
     here = Chip(sizes, shifts_ref)
     block_count = here.block_count
-    power = passed_ref[:HALO, :]
+    span = 2 * block_count
+    power = near[0][span : span + 1, :]
+    for ref in near[1:]:
+        power = power + ref[span : span + 1, :]
+    line = lax.broadcasted_iota(jnp.int32, (HALO, LANES), 0)
+    out_ref[:HALO, :] = jnp.where(line == 0, jnp.broadcast_to(power, (HALO, LANES)), 0.0)
+    for mask, ref in zip((0,) + NEAR_MASKS, near):
+        first[lines_at(HALO + ((here.chip ^ mask) & 3) * span, span), :] = ref[:span, :]
+    for pair in range(2):
+        at = HALO + 2 * pair * span
+        merge(first, at, at + span, here.delays(1, 2 * here.far + pair), second, at, block_count)
+    merge(second, HALO, HALO + 2 * span, here.delays(2, here.far), out_ref, HALO, block_count)
+
+
+def chip_levels(sizes, shifts_ref, near_ref, *refs):
+    merged, raw, (passed_ref, first, second) = refs[: len(FAR_MASKS)], refs[len(FAR_MASKS) : -3], refs[-3:]
+    here = Chip(sizes, shifts_ref)
+    block_count = here.block_count
+    span = 2 * block_count
+    line = lax.broadcasted_iota(jnp.int32, (HALO, LANES), 0)
+    end = len(RAW_MASKS) * block_count
+    passed_power = jnp.broadcast_to(passed_ref[end : end + 1, :], (HALO, LANES))
+    power = near_ref[:HALO, :] + jnp.where(line == 0, passed_power, 0.0)
     for number, (mask, ref) in enumerate(zip(RAW_MASKS, raw)):
-        base = HALO + 2 * number * block_count
+        base = HALO + number * span
         own, other = here.core * block_count, (1 - here.core) * block_count
         second[lines_at(base + own, block_count), :] = ref[HALO + block_count :, :]
-        at = HALO + number * block_count
+        at = number * block_count
         second[lines_at(base + other, block_count), :] = passed_ref[at : at + block_count, :]
-        delays = here.delays(0, here.chip ^ mask)
-        at = HALO + (here.chip ^ mask) * 2 * block_count
-        merge(second, base, base + block_count, delays, first, at, block_count)
+        at = HALO + ((here.chip ^ mask) & 3) * span
+        merge(second, base, base + block_count, here.delays(0, here.chip ^ mask), first, at, block_count)
         power = power + ref[:HALO, :]
-    for mask, ref in zip((0,) + MERGED_MASKS, merged):
-        first[lines_at(HALO + (here.chip ^ mask) * 2 * block_count, 2 * block_count), :] = ref[HALO:, :]
+    for mask, ref in zip(FAR_MASKS, merged):
+        first[lines_at(HALO + ((here.chip ^ mask) & 3) * span, span), :] = ref[HALO:, :]
         power = power + ref[:HALO, :]
-    for level in range(1, 3):
-        span = block_count << level
-        for group in range(8 >> level):
-            at = HALO + 2 * span * group
-            merge(first, at, at + span, here.delays(level, group), second, at, block_count)
-        first, second = second, first
-    return functools.partial(merge, first, HALO, HALO + 8 * block_count, here.delays(3, 0)), power
+    far = 1 - here.far
+    for pair in range(2):
+        at = HALO + 2 * pair * span
+        merge(first, at, at + span, here.delays(1, 2 * far + pair), second, at, block_count)
+    merge(second, HALO, HALO + 2 * span, here.delays(2, far), first, HALO + far * 4 * span, block_count)
+    first[lines_at(HALO + here.far * 4 * span, 4 * span), :] = near_ref[HALO:, :]
+    return functools.partial(merge, first, HALO, HALO + 4 * span, here.delays(3, 0)), power
 
 
 def packed_levels(sizes, low_bit, bit_count, shifts_ref, msg_ref, first, second):
@@ -355,6 +383,7 @@
 
     if stages[0] == 4 and row_count == 16:
         half = row_count // 2
+        near_shape = jax.ShapeDtypeStruct((2 * block_count + NEAR_LINES, LANES), jnp.float32)
         *raw, sent, kept = call(
             split_kernel,
             [lines(2)] * len(RAW_MASKS) + [lines(half, half + 1)] * 2,
@@ -366,18 +395,24 @@
         got = exchange(sent, 1)
         own, *merged = call(
             functools.partial(core_merge_kernel, block_count, row_count),
-            [lines(2)] * (1 + len(MERGED_MASKS)),
+            [near_shape] + [lines(2) if mask in FAR_MASKS else near_shape for mask in MERGED_MASKS],
             (shifts, got, kept),
         )
         merged = {mask: exchange(value, 2 * mask) for mask, value in zip(MERGED_MASKS, merged)}
         passed = call(
             functools.partial(pass_kernel, block_count),
-            lines(len(RAW_MASKS)),
+            near_shape,
             (*raw.values(), merged[PASS_AFTER]),
         )
         passed = exchange(passed, 1)
         after = own
-        messages = [own, *merged.values(), *raw.values(), passed]
+        near = call(
+            functools.partial(near_kernel, sizes),
+            lines(half),
+            (shifts, own, *(merged[mask] for mask in NEAR_MASKS)),
+            states,
+        )
+        messages = [near, *(merged[mask] for mask in FAR_MASKS), *raw.values(), passed]
         levels = functools.partial(chip_levels, sizes)
     else:
         packed = call(pack_kernel, lines(row_count, 1 << stages[0]), (spectra,), fetch, pltpu.HBM)

time: 22.1 us -> 22.4 us (1.014)
  Pallas kernels: 4.75 us -> 5.03 us
    pallas_call x5 -> x6, Pallas kernels: 4.75 us -> 5.03 us  [call(): pl.pallas_call(kernel, out_shape=out_shape, in_specs=[pl.BlockSpec(memory...]
  transfers between devices with their start and end apart: 9 -> 9, of which waited for: 3 -> 2; matrix products, arithmetic and copies ran while one was open for 0% -> 0% of each run, Pallas kernels for 2% -> 5%
where the time goes in v5:
time: 22.4 us; the launch traced here: 22.2 us
  starting transfers between devices  13.6 us (61%)
  Pallas kernels  5.03 us (22%)
  waiting for transfers between devices  3.44 us (15%)
    ppermute x9, starting transfers between devices, exchange(): lax.ppermute(value, 'freq', [(source, source ^ mask) for source in range(...  13.6 us
    pallas_call x6, Pallas kernels, call(): pl.pallas_call(kernel, out_shape=out_shape, in_specs=[pl.BlockSpec(memory...  5.03 us
    ppermute x9, waiting for transfers between devices, exchange(): lax.ppermute(value, 'freq', [(source, source ^ mask) for source in range(...  3.44 us
  transfers between devices with their start and end apart: 9, of which 2 were waited for; matrix products, arithmetic and copies ran while one was open for 0% of the time, Pallas kernels for 5%

profile of v5, /device:TPU:0, one launch (start us, length us, event | category | flops | bytes accessed | tf_op | source)
XLA Modules:
  0.0 22.2 jit_solution(5860348689836012788)
XLA Ops:
  0.0 0.0 copy-start
  0.0 1.2 %shard_map.37 = (f32[136,128]{1,0:T(8,128)S(1)}, f32[136,128]{1,0:T(8,128)S(1)}, f32[584,128]{1,0:T(8,128)S(1)}, f32[584,128]{1,0:T(8,128)S(1)}) custom-call(f32[16,8192]{1,0:T(8,128)} %x_ref.1), custom_call_target="tpu_custom_call" | custom-call | tf_op jit(solution)/shard_map/pallas_call | solution.py:347
  1.2 0.5 %collective-permute-start = (f32[584,128]{1,0:T(8,128)S(1)}, f32[584,128]{1,0:T(8,128)S(1)}, u32[]{:S(2)}, u32[]{:S(2)}) collective-permute-start(f32[584,128]{1,0:T(8,128)S(1)} %get-tuple-element.15), channel_id=1, source_target_pairs={{0,1},{1,0},{2,3},{3,2},{4,5},{5,4},{6,7},{7,6},{8,9},{9,8},{10,11... | collective-permute-start | bytes 897032 | tf_op jit(solution)/shard_map/ppermute | solution.py:342
  1.7 5.6 %collective-permute-start.6 = (f32[136,128]{1,0:T(8,128)S(1)}, f32[136,128]{1,0:T(8,128)S(1)}, u32[]{:S(2)}, u32[]{:S(2)}) collective-permute-start(f32[136,128]{1,0:T(8,128)S(1)} %get-tuple-element.23), channel_id=1, source_target_pairs={{0,14},{1,15},{2,12},{3,13},{4,10},{5,11},{6,8},{7,9},{8,6},{9,7},... | collective-permute-start | bytes 208904 | tf_op jit(solution)/shard_map/ppermute | solution.py:342
  7.3 0.0 collective-permute-start.7
  7.3 0.0 collective-permute-done.got_ref
  7.3 0.0 copy-done
  7.3 0.3 %shard_map.38 = (f32[135,128]{1,0:T(8,128)S(1)}, f32[136,128]{1,0:T(8,128)S(1)}, f32[136,128]{1,0:T(8,128)S(1)}, f32[135,128]{1,0:T(8,128)S(1)}, f32[135,128]{1,0:T(8,128)S(1)}, /*index=5*/f32[135,128]{1,0:T(8,128)S(1)}) custom-call(s32[15,32]{1,0:T(8,128)S(1)} %copy-done, f32[584,128]{1,0:T(8,128)S(1)} %collective-permute-done.got_ref, ...), custom_call_target="tpu_custom_call" | custom-call | tf_op jit(solution)/shard_map/pallas_call | solution.py:347
  7.7 1.7 %collective-permute-start.1 = (f32[135,128]{1,0:T(8,128)S(1)}, f32[135,128]{1,0:T(8,128)S(1)}, u32[]{:S(2)}, u32[]{:S(2)}) collective-permute-start(f32[135,128]{1,0:T(8,128)S(1)} %get-tuple-element.18), channel_id=1, source_target_pairs={{0,6},{1,7},{2,4},{3,5},{4,2},{5,3},{6,0},{7,1},{8,14},{9,15},{10,... | collective-permute-start | bytes 207368 | tf_op jit(solution)/shard_map/ppermute | solution.py:342
  9.4 1.7 %collective-permute-start.4 = (f32[136,128]{1,0:T(8,128)S(1)}, f32[136,128]{1,0:T(8,128)S(1)}, u32[]{:S(2)}, u32[]{:S(2)}) collective-permute-start(f32[136,128]{1,0:T(8,128)S(1)} %get-tuple-element.21), channel_id=1, source_target_pairs={{0,8},{1,9},{2,10},{3,11},{4,12},{5,13},{6,14},{7,15},{8,0},{9,1},... | collective-permute-start | bytes 208904 | tf_op jit(solution)/shard_map/ppermute | solution.py:342
  11.1 1.9 %collective-permute-start.5 = (f32[136,128]{1,0:T(8,128)S(1)}, f32[136,128]{1,0:T(8,128)S(1)}, u32[]{:S(2)}, u32[]{:S(2)}) collective-permute-start(f32[136,128]{1,0:T(8,128)S(1)} %get-tuple-element.22), channel_id=1, source_target_pairs={{0,12},{1,13},{2,14},{3,15},{4,8},{5,9},{6,10},{7,11},{8,4},{9,5},... | collective-permute-start | bytes 208904 | tf_op jit(solution)/shard_map/ppermute | solution.py:342
  13.0 0.0 collective-permute-done.6.refs_0_.refs_3_
  13.0 0.6 %collective-permute-start.2 = (f32[135,128]{1,0:T(8,128)S(1)}, f32[135,128]{1,0:T(8,128)S(1)}, u32[]{:S(2)}, u32[]{:S(2)}) collective-permute-start(f32[135,128]{1,0:T(8,128)S(1)} %get-tuple-element.19), channel_id=1, source_target_pairs={{0,4},{1,5},{2,6},{3,7},{4,0},{5,1},{6,2},{7,3},{8,12},{9,13},{10,... | collective-permute-start | bytes 207368 | tf_op jit(solution)/shard_map/ppermute | solution.py:342
  13.6 0.7 %collective-permute-done.7.refs_1_.refs_4_ = f32[136,128]{1,0:T(8,128)S(1)} collective-permute-done((f32[136,128]{1,0:T(8,128)S(1)}, f32[136,128]{1,0:T(8,128)S(1)}, u32[]{:S(2)}, u32[]{:S(2)}) %collective-permute-start.7) | collective-permute-done | bytes 69664 | tf_op jit(solution)/shard_map/ppermute | solution.py:342
  14.3 0.0 copy-start.1
  14.3 1.5 %collective-permute-start.3 = (f32[135,128]{1,0:T(8,128)S(1)}, f32[135,128]{1,0:T(8,128)S(1)}, u32[]{:S(2)}, u32[]{:S(2)}) collective-permute-start(f32[135,128]{1,0:T(8,128)S(1)} %get-tuple-element.20), channel_id=1, source_target_pairs={{0,2},{1,3},{2,0},{3,1},{4,6},{5,7},{6,4},{7,5},{8,10},{9,11},{10,... | collective-permute-start | bytes 207368 | tf_op jit(solution)/shard_map/ppermute | solution.py:342
  15.8 0.0 collective-permute-done.1.refs_1_.refs_2_
  15.8 0.1 collective-permute-start.8
  15.9 0.0 copy-done.1
  15.9 0.2 shard_map.39.table_ref
  16.1 2.7 %collective-permute-done.2.refs_2_ = f32[135,128]{1,0:T(8,128)S(1)} collective-permute-done((f32[135,128]{1,0:T(8,128)S(1)}, f32[135,128]{1,0:T(8,128)S(1)}, u32[]{:S(2)}, u32[]{:S(2)}) %collective-permute-start.2) | collective-permute-done | bytes 69152 | tf_op jit(solution)/shard_map/ppermute | solution.py:342
  18.8 0.0 collective-permute-done.3.refs_3_
  18.8 0.5 %shard_map.40.refs_0_ = f32[520,128]{1,0:T(8,128)S(1)} custom-call(s32[15,32]{1,0:T(8,128)S(1)} %copy-done, f32[135,128]{1,0:T(8,128)S(1)} %get-tuple-element.17.after_ref.refs_0_, f32[135,128]{1,0:T(8,128)S(1)} %collective-permute-done.1.refs_1_.refs_2_, f32[135,128]{1,0:T(8,128)S(1)} %collective-permute-done.2.refs_2_, ...), custom_call_target="tpu_custom_call" | custom-call | tf_op jit(solution)/shard_map/pallas_call | solution.py:347
  19.3 0.0 collective-permute-done.4.refs_1_
  19.3 0.0 collective-permute-done.5.refs_2_
  19.3 0.0 collective-permute-done.8.refs_5_
  19.3 2.9 %shard_map.42 = bf16[16,64,64]{2,1,0:T(8,128)(2,1)} custom-call(s32[15,32]{1,0:T(8,128)S(1)} %copy-done, bf16[1024,384]{1,0:T(8,128)(2,1)S(1)} %shard_map.39.table_ref, f32[520,128]{1,0:T(8,128)S(1)} %shard_map.40.refs_0_, f32[136,128]{1,0:T(8,128)S(1)} %collective-permute-done.4.refs_1_, f32[136,128]{1,0:T(8,128)S(1)} %collective-permute-done.5.refs_2_, ...), custom_call_target="tpu_custom_call" | custom-call | tf_op jit(solution)/shard_map/pallas_call | solution.py:347
  (1 shorter events, 0.0 us)
Async XLA Ops:
  0.0 7.3 %copy-start = (s32[15,32]{1,0:T(8,128)S(1)}, s32[15,32]{1,0:T(8,128)}, u32[]{:S(2)}) copy-start(s32[15,32]{1,0:T(8,128)} %shifts_ref.5) | copy-start | bytes 5764
  1.2 6.2 %collective-permute-start = (f32[584,128]{1,0:T(8,128)S(1)}, f32[584,128]{1,0:T(8,128)S(1)}, u32[]{:S(2)}, u32[]{:S(2)}) collective-permute-start(f32[584,128]{1,0:T(8,128)S(1)} %get-tuple-element.15), channel_id=1, source_target_pairs={{0,1},{1,0},{2,3},{3,2},{4,5},{5,4},{6,7},{7,6},{8,9},{9,8},{10,11... | collective-permute-start | bytes 897032 | tf_op jit(solution)/shard_map/ppermute | solution.py:342
  1.7 11.3 %collective-permute-start.6 = (f32[136,128]{1,0:T(8,128)S(1)}, f32[136,128]{1,0:T(8,128)S(1)}, u32[]{:S(2)}, u32[]{:S(2)}) collective-permute-start(f32[136,128]{1,0:T(8,128)S(1)} %get-tuple-element.23), channel_id=1, source_target_pairs={{0,14},{1,15},{2,12},{3,13},{4,10},{5,11},{6,8},{7,9},{8,6},{9,7},... | collective-permute-start | bytes 208904 | tf_op jit(solution)/shard_map/ppermute | solution.py:342
  7.3 7.0 %collective-permute-start.7 = (f32[136,128]{1,0:T(8,128)S(1)}, f32[136,128]{1,0:T(8,128)S(1)}, u32[]{:S(2)}, u32[]{:S(2)}) collective-permute-start(f32[136,128]{1,0:T(8,128)S(1)} %get-tuple-element.24), channel_id=1, source_target_pairs={{0,10},{1,11},{2,8},{3,9},{4,14},{5,15},{6,12},{7,13},{8,2},{9,3},... | collective-permute-start | bytes 208904 | tf_op jit(solution)/shard_map/ppermute | solution.py:342
  7.7 8.1 %collective-permute-start.1 = (f32[135,128]{1,0:T(8,128)S(1)}, f32[135,128]{1,0:T(8,128)S(1)}, u32[]{:S(2)}, u32[]{:S(2)}) collective-permute-start(f32[135,128]{1,0:T(8,128)S(1)} %get-tuple-element.18), channel_id=1, source_target_pairs={{0,6},{1,7},{2,4},{3,5},{4,2},{5,3},{6,0},{7,1},{8,14},{9,15},{10,... | collective-permute-start | bytes 207368 | tf_op jit(solution)/shard_map/ppermute | solution.py:342
  9.4 9.9 %collective-permute-start.4 = (f32[136,128]{1,0:T(8,128)S(1)}, f32[136,128]{1,0:T(8,128)S(1)}, u32[]{:S(2)}, u32[]{:S(2)}) collective-permute-start(f32[136,128]{1,0:T(8,128)S(1)} %get-tuple-element.21), channel_id=1, source_target_pairs={{0,8},{1,9},{2,10},{3,11},{4,12},{5,13},{6,14},{7,15},{8,0},{9,1},... | collective-permute-start | bytes 208904 | tf_op jit(solution)/shard_map/ppermute | solution.py:342
  11.1 8.2 %collective-permute-start.5 = (f32[136,128]{1,0:T(8,128)S(1)}, f32[136,128]{1,0:T(8,128)S(1)}, u32[]{:S(2)}, u32[]{:S(2)}) collective-permute-start(f32[136,128]{1,0:T(8,128)S(1)} %get-tuple-element.22), channel_id=1, source_target_pairs={{0,12},{1,13},{2,14},{3,15},{4,8},{5,9},{6,10},{7,11},{8,4},{9,5},... | collective-permute-start | bytes 208904 | tf_op jit(solution)/shard_map/ppermute | solution.py:342
  13.0 5.8 %collective-permute-start.2 = (f32[135,128]{1,0:T(8,128)S(1)}, f32[135,128]{1,0:T(8,128)S(1)}, u32[]{:S(2)}, u32[]{:S(2)}) collective-permute-start(f32[135,128]{1,0:T(8,128)S(1)} %get-tuple-element.19), channel_id=1, source_target_pairs={{0,4},{1,5},{2,6},{3,7},{4,0},{5,1},{6,2},{7,3},{8,12},{9,13},{10,... | collective-permute-start | bytes 207368 | tf_op jit(solution)/shard_map/ppermute | solution.py:342
  14.3 1.6 %copy-start.1 = (bf16[64,256]{1,0:T(8,128)(2,1)S(1)}, bf16[64,256]{1,0:T(8,128)(2,1)}, u32[]{:S(2)}) copy-start(bf16[64,256]{1,0:T(8,128)(2,1)} %prof_ref.1) | copy-start | bytes 98308
  14.3 4.5 %collective-permute-start.3 = (f32[135,128]{1,0:T(8,128)S(1)}, f32[135,128]{1,0:T(8,128)S(1)}, u32[]{:S(2)}, u32[]{:S(2)}) collective-permute-start(f32[135,128]{1,0:T(8,128)S(1)} %get-tuple-element.20), channel_id=1, source_target_pairs={{0,2},{1,3},{2,0},{3,1},{4,6},{5,7},{6,4},{7,5},{8,10},{9,11},{10,... | collective-permute-start | bytes 207368 | tf_op jit(solution)/shard_map/ppermute | solution.py:342
  15.8 3.5 %collective-permute-start.8 = (f32[135,128]{1,0:T(8,128)S(1)}, f32[135,128]{1,0:T(8,128)S(1)}, u32[]{:S(2)}, u32[]{:S(2)}) collective-permute-start(f32[135,128]{1,0:T(8,128)S(1)} %shard_map.41), channel_id=1, source_target_pairs={{0,1},{1,0},{2,3},{3,2},{4,5},{5,4},{6,7},{7,6},{8,9},{9,8},{10,11... | collective-permute-start | bytes 207368 | tf_op jit(solution)/shard_map/ppermute | solution.py:342

commit v6 on v3

--- a/solution.py
+++ b/solution.py
@@ -26,6 +26,8 @@
 
 
 def lines_at(start, count):
+    if isinstance(start, int):
+        return slice(start, start + count)
     return pl.ds(pl.multiple_of(start, 8), count)
 
 

time: 22.1 us -> 22.1 us (level)
  no operation moved by 1% of the time
where the time goes in v6:
time: 22.1 us; the launch traced here: 21.9 us
  starting transfers between devices  13.6 us (62%)
  Pallas kernels  4.77 us (22%)
  waiting for transfers between devices  3.44 us (16%)
    ppermute x9, starting transfers between devices, exchange(): lax.ppermute(value, 'freq', [(source, source ^ mask) for source in range(...  13.6 us
    pallas_call x5, Pallas kernels, call(): pl.pallas_call(kernel, out_shape=out_shape, in_specs=[pl.BlockSpec(memory...  4.77 us
    ppermute x9, waiting for transfers between devices, exchange(): lax.ppermute(value, 'freq', [(source, source ^ mask) for source in range(...  3.44 us
  transfers between devices with their start and end apart: 9, of which 3 were waited for; matrix products, arithmetic and copies ran while one was open for 0% of the time, Pallas kernels for 2%

profile of v6, /device:TPU:0, one launch (start us, length us, event | category | flops | bytes accessed | tf_op | source)
XLA Modules:
  0.0 21.9 jit_solution(4478085893106250852)
XLA Ops:
  0.0 0.0 copy-start
  0.0 1.2 %shard_map.37 = (f32[136,128]{1,0:T(8,128)S(1)}, f32[136,128]{1,0:T(8,128)S(1)}, f32[520,128]{1,0:T(8,128)S(1)}, f32[520,128]{1,0:T(8,128)S(1)}) custom-call(f32[16,8192]{1,0:T(8,128)} %x_ref.1), custom_call_target="tpu_custom_call" | custom-call | tf_op jit(solution)/shard_map/pallas_call | solution.py:310
  1.2 0.5 %collective-permute-start = (f32[520,128]{1,0:T(8,128)S(1)}, f32[520,128]{1,0:T(8,128)S(1)}, u32[]{:S(2)}, u32[]{:S(2)}) collective-permute-start(f32[520,128]{1,0:T(8,128)S(1)} %get-tuple-element.15), channel_id=1, source_target_pairs={{0,1},{1,0},{2,3},{3,2},{4,5},{5,4},{6,7},{7,6},{8,9},{9,8},{10,11... | collective-permute-start | bytes 798728 | tf_op jit(solution)/shard_map/ppermute | solution.py:305
  1.7 5.6 %collective-permute-start.6 = (f32[136,128]{1,0:T(8,128)S(1)}, f32[136,128]{1,0:T(8,128)S(1)}, u32[]{:S(2)}, u32[]{:S(2)}) collective-permute-start(f32[136,128]{1,0:T(8,128)S(1)} %get-tuple-element.23), channel_id=1, source_target_pairs={{0,14},{1,15},{2,12},{3,13},{4,10},{5,11},{6,8},{7,9},{8,6},{9,7},... | collective-permute-start | bytes 208904 | tf_op jit(solution)/shard_map/ppermute | solution.py:305
  7.4 0.0 collective-permute-start.7
  7.4 0.0 collective-permute-done.got_ref
  7.4 0.0 copy-done
  7.4 0.3 %shard_map.38 = (f32[136,128]{1,0:T(8,128)S(1)}, f32[136,128]{1,0:T(8,128)S(1)}, f32[136,128]{1,0:T(8,128)S(1)}, f32[136,128]{1,0:T(8,128)S(1)}, f32[136,128]{1,0:T(8,128)S(1)}, /*index=5*/f32[136,128]{1,0:T(8,128)S(1)}) custom-call(s32[15,32]{1,0:T(8,128)S(1)} %copy-done, f32[520,128]{1,0:T(8,128)S(1)} %collective-permute-done.got_ref, ...), custom_call_target="tpu_custom_call" | custom-call | tf_op jit(solution)/shard_map/pallas_call | solution.py:310
  7.7 1.7 %collective-permute-start.3 = (f32[136,128]{1,0:T(8,128)S(1)}, f32[136,128]{1,0:T(8,128)S(1)}, u32[]{:S(2)}, u32[]{:S(2)}) collective-permute-start(f32[136,128]{1,0:T(8,128)S(1)} %get-tuple-element.20), channel_id=1, source_target_pairs={{0,6},{1,7},{2,4},{3,5},{4,2},{5,3},{6,0},{7,1},{8,14},{9,15},{10,... | collective-permute-start | bytes 208904 | tf_op jit(solution)/shard_map/ppermute | solution.py:305
  9.4 1.7 %collective-permute-start.1 = (f32[136,128]{1,0:T(8,128)S(1)}, f32[136,128]{1,0:T(8,128)S(1)}, u32[]{:S(2)}, u32[]{:S(2)}) collective-permute-start(f32[136,128]{1,0:T(8,128)S(1)} %get-tuple-element.18), channel_id=1, source_target_pairs={{0,8},{1,9},{2,10},{3,11},{4,12},{5,13},{6,14},{7,15},{8,0},{9,1},... | collective-permute-start | bytes 208904 | tf_op jit(solution)/shard_map/ppermute | solution.py:305
  11.1 1.9 %collective-permute-start.2 = (f32[136,128]{1,0:T(8,128)S(1)}, f32[136,128]{1,0:T(8,128)S(1)}, u32[]{:S(2)}, u32[]{:S(2)}) collective-permute-start(f32[136,128]{1,0:T(8,128)S(1)} %get-tuple-element.19), channel_id=1, source_target_pairs={{0,12},{1,13},{2,14},{3,15},{4,8},{5,9},{6,10},{7,11},{8,4},{9,5},... | collective-permute-start | bytes 208904 | tf_op jit(solution)/shard_map/ppermute | solution.py:305
  13.0 0.0 collective-permute-done.6.refs_0_.refs_6_
  13.0 0.6 %collective-permute-start.4 = (f32[136,128]{1,0:T(8,128)S(1)}, f32[136,128]{1,0:T(8,128)S(1)}, u32[]{:S(2)}, u32[]{:S(2)}) collective-permute-start(f32[136,128]{1,0:T(8,128)S(1)} %get-tuple-element.21), channel_id=1, source_target_pairs={{0,4},{1,5},{2,6},{3,7},{4,0},{5,1},{6,2},{7,3},{8,12},{9,13},{10,... | collective-permute-start | bytes 208904 | tf_op jit(solution)/shard_map/ppermute | solution.py:305
  13.6 0.7 %collective-permute-done.7.refs_1_.refs_7_ = f32[136,128]{1,0:T(8,128)S(1)} collective-permute-done((f32[136,128]{1,0:T(8,128)S(1)}, f32[136,128]{1,0:T(8,128)S(1)}, u32[]{:S(2)}, u32[]{:S(2)}) %collective-permute-start.7) | collective-permute-done | bytes 69664 | tf_op jit(solution)/shard_map/ppermute | solution.py:305
  14.3 0.0 copy-start.1
  14.3 1.5 %collective-permute-start.5 = (f32[136,128]{1,0:T(8,128)S(1)}, f32[136,128]{1,0:T(8,128)S(1)}, u32[]{:S(2)}, u32[]{:S(2)}) collective-permute-start(f32[136,128]{1,0:T(8,128)S(1)} %get-tuple-element.22), channel_id=1, source_target_pairs={{0,2},{1,3},{2,0},{3,1},{4,6},{5,7},{6,4},{7,5},{8,10},{9,11},{10,... | collective-permute-start | bytes 208904 | tf_op jit(solution)/shard_map/ppermute | solution.py:305
  15.8 0.0 collective-permute-done.3.refs_2_.refs_3_
  15.8 0.1 collective-permute-start.8
  15.9 0.0 copy-done.1
  15.9 0.2 shard_map.39.table_ref
  16.1 2.6 %collective-permute-done.1.refs_1_ = f32[136,128]{1,0:T(8,128)S(1)} collective-permute-done((f32[136,128]{1,0:T(8,128)S(1)}, f32[136,128]{1,0:T(8,128)S(1)}, u32[]{:S(2)}, u32[]{:S(2)}) %collective-permute-start.1) | collective-permute-done | bytes 69664 | tf_op jit(solution)/shard_map/ppermute | solution.py:305
  18.8 0.0 collective-permute-done.2.refs_2_
  18.8 0.1 collective-permute-done.4.refs_4_
  18.8 0.0 collective-permute-done.5.refs_5_
  18.8 0.0 collective-permute-done.8.refs_8_
  18.8 3.0 %shard_map.41 = bf16[16,64,64]{2,1,0:T(8,128)(2,1)} custom-call(s32[15,32]{1,0:T(8,128)S(1)} %copy-done, bf16[1024,384]{1,0:T(8,128)(2,1)S(1)} %shard_map.39.table_ref, f32[136,128]{1,0:T(8,128)S(1)} %get-tuple-element.17.after_ref.refs_0_, f32[136,128]{1,0:T(8,128)S(1)} %collective-permute-done.1.refs_1_, f32[136,128]{1,0:T(8,128)S(1)} %collective-permute-done.2.refs_2_, ...), custom_call_target="tpu_custom_call" | custom-call | tf_op jit(solution)/shard_map/pallas_call | solution.py:310
  (1 shorter events, 0.0 us)
Async XLA Ops:
  0.0 7.4 %copy-start = (s32[15,32]{1,0:T(8,128)S(1)}, s32[15,32]{1,0:T(8,128)}, u32[]{:S(2)}) copy-start(s32[15,32]{1,0:T(8,128)} %shifts_ref.3) | copy-start | bytes 5764
  1.2 6.2 %collective-permute-start = (f32[520,128]{1,0:T(8,128)S(1)}, f32[520,128]{1,0:T(8,128)S(1)}, u32[]{:S(2)}, u32[]{:S(2)}) collective-permute-start(f32[520,128]{1,0:T(8,128)S(1)} %get-tuple-element.15), channel_id=1, source_target_pairs={{0,1},{1,0},{2,3},{3,2},{4,5},{5,4},{6,7},{7,6},{8,9},{9,8},{10,11... | collective-permute-start | bytes 798728 | tf_op jit(solution)/shard_map/ppermute | solution.py:305
  1.7 11.3 %collective-permute-start.6 = (f32[136,128]{1,0:T(8,128)S(1)}, f32[136,128]{1,0:T(8,128)S(1)}, u32[]{:S(2)}, u32[]{:S(2)}) collective-permute-start(f32[136,128]{1,0:T(8,128)S(1)} %get-tuple-element.23), channel_id=1, source_target_pairs={{0,14},{1,15},{2,12},{3,13},{4,10},{5,11},{6,8},{7,9},{8,6},{9,7},... | collective-permute-start | bytes 208904 | tf_op jit(solution)/shard_map/ppermute | solution.py:305
  7.4 7.0 %collective-permute-start.7 = (f32[136,128]{1,0:T(8,128)S(1)}, f32[136,128]{1,0:T(8,128)S(1)}, u32[]{:S(2)}, u32[]{:S(2)}) collective-permute-start(f32[136,128]{1,0:T(8,128)S(1)} %get-tuple-element.24), channel_id=1, source_target_pairs={{0,10},{1,11},{2,8},{3,9},{4,14},{5,15},{6,12},{7,13},{8,2},{9,3},... | collective-permute-start | bytes 208904 | tf_op jit(solution)/shard_map/ppermute | solution.py:305
  7.7 8.1 %collective-permute-start.3 = (f32[136,128]{1,0:T(8,128)S(1)}, f32[136,128]{1,0:T(8,128)S(1)}, u32[]{:S(2)}, u32[]{:S(2)}) collective-permute-start(f32[136,128]{1,0:T(8,128)S(1)} %get-tuple-element.20), channel_id=1, source_target_pairs={{0,6},{1,7},{2,4},{3,5},{4,2},{5,3},{6,0},{7,1},{8,14},{9,15},{10,... | collective-permute-start | bytes 208904 | tf_op jit(solution)/shard_map/ppermute | solution.py:305
  9.4 9.3 %collective-permute-start.1 = (f32[136,128]{1,0:T(8,128)S(1)}, f32[136,128]{1,0:T(8,128)S(1)}, u32[]{:S(2)}, u32[]{:S(2)}) collective-permute-start(f32[136,128]{1,0:T(8,128)S(1)} %get-tuple-element.18), channel_id=1, source_target_pairs={{0,8},{1,9},{2,10},{3,11},{4,12},{5,13},{6,14},{7,15},{8,0},{9,1},... | collective-permute-start | bytes 208904 | tf_op jit(solution)/shard_map/ppermute | solution.py:305
  11.1 7.7 %collective-permute-start.2 = (f32[136,128]{1,0:T(8,128)S(1)}, f32[136,128]{1,0:T(8,128)S(1)}, u32[]{:S(2)}, u32[]{:S(2)}) collective-permute-start(f32[136,128]{1,0:T(8,128)S(1)} %get-tuple-element.19), channel_id=1, source_target_pairs={{0,12},{1,13},{2,14},{3,15},{4,8},{5,9},{6,10},{7,11},{8,4},{9,5},... | collective-permute-start | bytes 208904 | tf_op jit(solution)/shard_map/ppermute | solution.py:305
  13.0 5.8 %collective-permute-start.4 = (f32[136,128]{1,0:T(8,128)S(1)}, f32[136,128]{1,0:T(8,128)S(1)}, u32[]{:S(2)}, u32[]{:S(2)}) collective-permute-start(f32[136,128]{1,0:T(8,128)S(1)} %get-tuple-element.21), channel_id=1, source_target_pairs={{0,4},{1,5},{2,6},{3,7},{4,0},{5,1},{6,2},{7,3},{8,12},{9,13},{10,... | collective-permute-start | bytes 208904 | tf_op jit(solution)/shard_map/ppermute | solution.py:305
  14.3 1.6 %copy-start.1 = (bf16[64,256]{1,0:T(8,128)(2,1)S(1)}, bf16[64,256]{1,0:T(8,128)(2,1)}, u32[]{:S(2)}) copy-start(bf16[64,256]{1,0:T(8,128)(2,1)} %prof_ref.1) | copy-start | bytes 98308
  14.3 4.5 %collective-permute-start.5 = (f32[136,128]{1,0:T(8,128)S(1)}, f32[136,128]{1,0:T(8,128)S(1)}, u32[]{:S(2)}, u32[]{:S(2)}) collective-permute-start(f32[136,128]{1,0:T(8,128)S(1)} %get-tuple-element.22), channel_id=1, source_target_pairs={{0,2},{1,3},{2,0},{3,1},{4,6},{5,7},{6,4},{7,5},{8,10},{9,11},{10,... | collective-permute-start | bytes 208904 | tf_op jit(solution)/shard_map/ppermute | solution.py:305
  15.8 3.0 %collective-permute-start.8 = (f32[136,128]{1,0:T(8,128)S(1)}, f32[136,128]{1,0:T(8,128)S(1)}, u32[]{:S(2)}, u32[]{:S(2)}) collective-permute-start(f32[136,128]{1,0:T(8,128)S(1)} %shard_map.40), channel_id=1, source_target_pairs={{0,1},{1,0},{2,3},{3,2},{4,5},{5,4},{6,7},{7,6},{8,9},{9,8},{10,11... | collective-permute-start | bytes 208904 | tf_op jit(solution)/shard_map/ppermute | solution.py:305
